TPU v7x, 128 devices: a whole 4x4x4 slice. The times are simulated.
128 devices in a mesh: dp: 16 (over z, x_lo, core), mic: 8 (over x_hi, y).
Axes of the slice: x: 4 (x_hi: 2, x_lo: 2; x = x_hi * 2 + x_lo), y: 4, z: 4, core: 2. Of those that a mesh axis runs over, the one named last changes fastest.
Arguments:
- waveform: bfloat16 [2, 32, 65536], P(None, 'mic', 'dp'), may hold values from -12 to 12
- filters: bfloat16 [512, 32], P('mic'), may hold values from -1 to 1
- speech_mask: bfloat16 [2, 256, 4096], P(None, 'mic', 'dp'), may hold values from 0.049804688 to 1
- noise_mask: bfloat16 [2, 256, 4096], P(None, 'mic', 'dp'), may hold values from 0.049804688 to 1
- target: float32 [2, 2, 256, 4096], P(None, None, 'mic', 'dp'), may hold values from -6 to 6
- ref_mic: int32 [2], replicated, may hold values from 0 to 31
Outputs:
- enhanced: float32 [2, 2, 256, 4096], P(None, None, 'mic', 'dp')
- filter_grad: float32 [512, 32], P('mic')
All inputs are finite; a program needn't handle non-finite values.
Results may differ from a plain program's by a relative error of at most 0.015.
Values may be sent and summed in bfloat16 or wider, within the bound.
A program may use at most 128 MiB of HBM per device.

v0:
```python
import jax
import jax.numpy as jnp
from jax import lax
from jax.sharding import PartitionSpec as P

FILTERS = 512
STRIDE = 16
MICS = 32
FREQS = 256


LOAD_NOISE = 0.05
LOAD_SPEECH = 0.05
LOSS_SCALE = 64.0


def passed_along(block, axis, distance):
    devices = range(lax.axis_size(axis))
    route = [(i - distance, i) for i in devices if i - distance in devices]
    return lax.ppermute(block, axis, route)


def frame_signal(extended):
    batch, mic_count, samples = extended.shape
    block_count = samples // STRIDE
    pieces = jnp.swapaxes(extended.reshape(batch, mic_count, block_count, STRIDE), 2, 3)
    return jnp.concatenate([pieces[..., :-1], pieces[..., 1:]], axis=2)


def encode_rows(filter_rows, frames):
    return jnp.einsum(
        "rk,bmkt->brmt", filter_rows, frames, preferred_element_type=jnp.float32
    ).astype(jnp.bfloat16)


def complex_parts(gram):
    mic_count = gram.shape[-1] // 2
    real_sum = gram[..., :mic_count, :mic_count] + gram[..., mic_count:, mic_count:]
    imag_sum = gram[..., mic_count:, :mic_count] - gram[..., :mic_count, mic_count:]
    return (real_sum, imag_sum)


def real_form(real_sum, imag_sum):
    top_rows = jnp.concatenate([real_sum, -imag_sum], axis=-1)
    bottom = jnp.concatenate([imag_sum, real_sum], axis=-1)
    return jnp.concatenate([top_rows, bottom], axis=-2)


def beam_weights(onehot, frame_total, speech_real, speech_imag, noise_real, noise_imag):
    mic_count = speech_real.shape[-1]
    identity = jnp.eye(2 * mic_count, dtype=jnp.float32)
    noise_cov = real_form(noise_real, noise_imag) / frame_total + LOAD_NOISE * identity
    speech_cols = (
        jnp.concatenate([speech_real, speech_imag], axis=-2) / frame_total
        + LOAD_SPEECH * identity[:, :mic_count]
    )
    factor = jnp.linalg.cholesky(noise_cov)
    halfway = jax.scipy.linalg.solve_triangular(factor, speech_cols, lower=True)
    ratios = jax.scipy.linalg.solve_triangular(factor, halfway, lower=True, trans=1)
    trace_sum = jnp.trace(ratios[..., :mic_count, :], axis1=-2, axis2=-1)
    column = (
        jnp.einsum("bfim,bm->bfi", ratios, onehot, precision=lax.Precision.HIGHEST)
        / trace_sum[..., None]
    )
    real_part = column[..., :mic_count]
    imag_part = column[..., mic_count:]
    first_row = jnp.concatenate([real_part, imag_part], axis=-1)
    second = jnp.concatenate([-imag_part, real_part], axis=-1)
    return jnp.stack([first_row, second], axis=-2)


def local(waveform, filters, speech_mask, noise_mask, target, ref_mic):
    highest = lax.Precision.HIGHEST
    batch = waveform.shape[0]
    freq_local = speech_mask.shape[1]
    frame_count = speech_mask.shape[2]
    frame_total = float(frame_count * lax.axis_size("dp"))
    tail = passed_along(waveform[:, :, :STRIDE], "dp", -1)
    extended = jnp.concatenate([waveform, tail], axis=2)
    every_filter = lax.all_gather(filters, "mic", axis=0, tiled=True)
    frames = frame_signal(extended)
    local_rows = encode_rows(every_filter, frames)
    shaped = local_rows.reshape(batch, FREQS, 2, local_rows.shape[2], frame_count)
    moved = lax.all_to_all(shaped, "mic", split_axis=1, concat_axis=3, tiled=True)
    stacked = moved.reshape(batch, freq_local, 2 * MICS, frame_count)
    onehot = (jnp.arange(MICS, dtype=jnp.int32)[None, :] == ref_mic[:, None]).astype(jnp.float32)

    def weigh(speech_real, speech_imag, noise_real, noise_imag):
        return beam_weights(onehot, frame_total, speech_real, speech_imag, noise_real, noise_imag)

    speech_part = stacked * speech_mask[:, :, None, :]
    noise_part = stacked * noise_mask[:, :, None, :]
    speech_gram = jnp.einsum(
        "bfit,bfjt->bfij", speech_part, stacked, preferred_element_type=jnp.float32
    )
    noise_gram = jnp.einsum(
        "bfit,bfjt->bfij", noise_part, stacked, preferred_element_type=jnp.float32
    )
    statistics = jnp.stack([speech_gram, noise_gram], axis=2)
    summed = lax.psum(statistics, "dp")
    sums = complex_parts(summed[:, :, 0]) + complex_parts(summed[:, :, 1])
    own_weights, pullback = jax.vjp(weigh, sums[0], sums[1], sums[2], sums[3])
    stacked_wide = stacked.astype(jnp.float32)
    enhanced = jnp.einsum("bfvi,bfit->bvft", own_weights, stacked_wide, precision=highest)
    grad_scale = 2.0 * LOSS_SCALE / (batch * FREQS * frame_total)
    enhanced_grad = grad_scale * (enhanced - target)
    beam_part = jnp.einsum("bvft,bfit->bfvi", enhanced_grad, stacked_wide, precision=highest)
    beam_grad = lax.psum(beam_part, "dp")
    part_grads = pullback(beam_grad)
    speech_grad = real_form(part_grads[0], part_grads[1])
    noise_grad = real_form(part_grads[2], part_grads[3])
    speech_wide = speech_part.astype(jnp.float32)
    noise_wide = noise_part.astype(jnp.float32)
    stacked_grad = jnp.einsum("bfvi,bvft->bfit", own_weights, enhanced_grad, precision=highest)
    stacked_grad = stacked_grad + speech_mask[:, :, None, :] * jnp.einsum(
        "bfij,bfjt->bfit", speech_grad, stacked_wide, precision=highest
    )
    stacked_grad = stacked_grad + jnp.einsum(
        "bfji,bfjt->bfit", speech_grad, speech_wide, precision=highest
    )
    stacked_grad = stacked_grad + noise_mask[:, :, None, :] * jnp.einsum(
        "bfij,bfjt->bfit", noise_grad, stacked_wide, precision=highest
    )
    stacked_grad = stacked_grad + jnp.einsum(
        "bfji,bfjt->bfit", noise_grad, noise_wide, precision=highest
    )
    stacked_grad = stacked_grad.astype(jnp.bfloat16)
    shaped_grad = stacked_grad.reshape(batch, freq_local, 2, MICS, frame_count)
    returned = lax.all_to_all(shaped_grad, "mic", split_axis=3, concat_axis=1, tiled=True)
    local_grad = returned.reshape(batch, FILTERS, returned.shape[3], frame_count)
    own_rows = lax.psum_scatter(
        jnp.einsum("brmt,bmkt->rk", local_grad, frames, preferred_element_type=jnp.float32),
        "mic",
        scatter_dimension=0,
        tiled=True,
    )
    filter_grad = lax.psum(own_rows, "dp")
    return (enhanced, filter_grad)


def solution(mesh):
    in_specs = (
        P(None, "mic", "dp"),
        P("mic", None),
        P(None, "mic", "dp"),
        P(None, "mic", "dp"),
        P(None, None, "mic", "dp"),
        P(),
    )
    out_specs = (P(None, None, "mic", "dp"), P("mic", None))
    return jax.shard_map(local, mesh=mesh, in_specs=in_specs, out_specs=out_specs, check_vma=False)
```

profile of v0, /device:TPU:1, one launch (start us, length us, event | category | flops | bytes accessed | tf_op | source)
XLA Modules:
  0.0 1265.8 jit_solution(2961033993358371283)
XLA Ops:
  11.2 29.2 %all-gather = bf16[8,64,32]{1,2,0:T(8,128)(2,1)S(1)} all-gather(bf16[1,64,32]{1,2,0:T(8,128)(2,1)} %bitcast.124), channel_id=1, replica_groups=mesh['dp'=16,'mic'=8] {'mic'}, dimensions={0}, use_global_device_ids=true | all-gather | bytes 36864 | tf_op jit(solution)/shard_map/all_gather | solution.py:80
  48.4 27.1 %all_to_all.30 = bf16[2,256,2,4,256]{4,3,2,0,1:T(4,128)(2,1)S(1)} all-to-all(bf16[2,256,2,4,256]{4,3,2,0,1:T(4,128)(2,1)S(1)} %copy.111), channel_id=1, replica_groups=mesh['dp'=16,'mic'=8] {'mic'}, dimensions={1} | all-to-all | bytes 4194304 | tf_op jit(solution)/shard_map/all_to_all | solution.py:84
  87.7 136.9 %all-reduce.5.cloned.1.call-done = f32[2,32,2,64,64]{3,4,1,0,2:T(8,128)} async-done(((f32[2,32,2,64,64]{3,4,1,0,2:T(8,128)}), f32[2,32,2,64,64]{3,4,1,0,2:T(8,128)}) %all-reduce.5.cloned.1.call-update) | async-done | bytes 2097168 | tf_op jit(solution)/shard_map/psum | solution.py:100
  240.2 376.9 %custom-call.17 = f32[2,32,64,64]{3,2,1,0:T(8,128)} custom-call(f32[2,32,64,64]{3,2,1,0:T(8,128)} %fusion.13), custom_call_target="Cholesky" | custom-call | tf_op jit(solution)/shard_map/jvp(jit(cholesky))/cholesky | solution.py:57
  632.1 5.2 copy.133
  637.4 134.0 %custom-call.22 = f32[2,32,1,64,64]{1,3,4,2,0:T(8,128)} custom-call(f32[2,32,1,64,64]{1,4,3,2,0:T(8,128)} %select_bitcast_fusion), custom_call_target="InvertDiagBlocksLowerTriangular" | custom-call | tf_op jit(solution)/shard_map/jvp(jit(_solve_triangular))/vmap(vmap())/triangular_solve/custom-call.2 | solution.py:59
  771.3 5.9 copy.122
  777.2 5.6 fusion.23
  789.8 54.6 %psum.22 = f32[2,32,2,64]{3,1,0,2:T(8,128)} all-reduce(f32[2,32,2,64]{3,1,0,2:T(8,128)} %copy.127), channel_id=1, replica_groups=mesh['dp'=16,'mic'=8] {'dp'}, use_global_device_ids=true, to_apply=%region_4.7 | all-reduce | flops 8192 | bytes 65536 | tf_op jit(solution)/shard_map/psum | solution.py:108
  846.3 5.3 fusion.27
  859.9 134.0 %custom-call.18 = f32[2,32,1,64,64]{1,3,4,2,0:T(8,128)} custom-call(f32[2,32,1,64,64]{1,4,3,2,0:T(8,128)} %get-tuple-element.14), custom_call_target="InvertDiagBlocksLowerTriangular" | custom-call | tf_op jit(solution)/shard_map/transpose(jvp(jit(cholesky)))/triangular_solve | solution.py:57
  993.9 5.6 copy.139
  999.5 6.2 fusion.67
  1013.4 5.6 add_select_fusion
  1023.1 5.8 fusion.68
  1032.8 5.2 divide_select_fusion
  1042.5 5.8 fusion.69
  1051.9 5.6 copy.140
  1061.4 5.3 fusion.42
  1081.6 5.4 copy.144
  1090.9 6.8 add_convert_fusion
  1099.9 28.8 %all_to_all.31 = bf16[2,32,2,32,256]{4,2,1,0,3:T(2,128)(2,1)S(1)} all-to-all(bf16[2,32,2,32,256]{4,2,1,0,3:T(2,128)(2,1)S(1)} %copy.145), channel_id=1, replica_groups=mesh['dp'=16,'mic'=8] {'mic'}, dimensions={3} | all-to-all | bytes 4194304 | tf_op jit(solution)/shard_map/all_to_all | solution.py:129
  1136.4 69.6 %reduce-scatter.4.cloned.1.call-done = f32[64,32]{1,0:T(8,128)} async-done(((f32[512,32]{1,0:T(8,128)}), f32[64,32]{1,0:T(8,128)}) %reduce-scatter.4.cloned.1.call-update) | async-done | bytes 8208
  1206.9 51.9 %psum.23 = f32[64,32]{0,1:T(8,128)} all-reduce(f32[64,32]{0,1:T(8,128)S(1)} %copy.156), channel_id=1, replica_groups=mesh['dp'=16,'mic'=8] {'dp'}, use_global_device_ids=true, to_apply=%region_7.10 | all-reduce | flops 2048 | bytes 16384 | tf_op jit(solution)/shard_map/psum | solution.py:137
  (138 shorter events, 128.9 us)
Async XLA Ops:
  7.2 217.4 %all-reduce.5.cloned.1.call-start = ((), (), s32[]{:S(2)}) async-start(), calls=%async_computation.3 | async-start | bytes 8388608 | tf_op jit(solution)/shard_map/psum | solution.py:100
  7.9 32.6 %collective-permute-start = (bf16[2,4,16]{2,1,0:T(4,128)(2,1)S(1)}, bf16[2,4,16]{2,1,0:T(4,128)(2,1)S(1)}, u32[]{:S(2)}, u32[]{:S(2)}) collective-permute-start(bf16[2,4,16]{2,1,0:T(4,128)(2,1)S(1)} %slice.78), channel_id=1, source_target_pairs={{8,0},{16,8},{24,16},{32,24},{40,32},{48,40},{56,48},{64,56},{72,6... | collective-permute-start | bytes 776 | tf_op jit(solution)/shard_map/ppermute | solution.py:20
  78.0 2.6 copy-start.16
  84.6 1121.5 %reduce-scatter.4.cloned.1.call-start = ((), (), s32[]{:S(2)}) async-start(), calls=%async_computation.4 | async-start | bytes 294912
  621.0 3.5 copy-start.3
  771.3 5.9 copy-start.14
  777.2 5.6 copy-start
  782.9 2.0 copy-start.10
  785.3 2.2 copy-start.22
  846.3 5.3 copy-start.1
  993.9 5.6 copy-start.11
  1042.5 5.8 copy-start.4
  1057.5 3.9 copy-start.23
  1061.4 5.3 copy-start.9
  1071.2 4.6 copy-start.6
  1071.2 4.6 copy-start.7
  1071.2 4.6 copy-start.24
  1071.2 4.6 copy-start.25
  1071.2 4.6 copy-start.26
  1087.1 3.8 copy-start.5
  1087.1 3.8 copy-start.8
  1087.1 3.8 copy-start.17
  1130.5 2.2 copy-start.19
  1130.5 2.2 copy-start.21
  (7 other events, 8.1 us)
Sparse Core Ops, SparseCore 0:
  84.7 139.8 all-reduce.4
  1135.9 70.1 reduce-scatter.3
where the time goes:
time: 1270 us
  other arithmetic  687 us (54%)
  waiting for transfers between devices  207 us (16%)
  blocking collectives  192 us (15%)
  local copies, waits for them, and re-layouts  86.6 us (7%)
  matrix products  75.4 us (6%)
  between operations  14.8 us (1%)
    another operation x6, other arithmetic, beam_weights(): factor = jnp.linalg.cholesky(noise_cov)  517 us
    another operation x3, other arithmetic, beam_weights(): jax.scipy.linalg.solve_triangular(factor, halfway, lower=True, trans=1)  137 us
    psum x1, waiting for transfers between devices, local(): summed = lax.psum(statistics, 'dp')  137 us
    unnamed x3, waiting for transfers between devices  69.7 us
    psum x1, blocking collectives, local(): beam_grad = lax.psum(beam_part, 'dp')  54.6 us
    psum x1, blocking collectives, local(): filter_grad = lax.psum(own_rows, 'dp')  51.9 us
    all_gather x1, blocking collectives, local(): every_filter = lax.all_gather(filters, 'mic', axis=0, tiled=True)  29.2 us
    all_to_all x1, blocking collectives, local(): lax.all_to_all(shaped_grad, 'mic', split_axis=3, concat_axis=1, tiled=True)  28.8 us
  transfers between devices with their start and end apart: 3, of which 2 were waited for; matrix products, arithmetic and copies ran while one was open for 0% of the time, Pallas kernels for 0%

commit v1 on v0

v1 whole, which is shorter than its diff:
```python
import jax
import jax.numpy as jnp
from jax import lax
from jax.experimental import pallas as pl
from jax.experimental.pallas import tpu as pltpu
from jax.sharding import PartitionSpec as P

DP = 16
MIC = 8
MICS = 32
TD = 256
LOAD = 0.05
FRAME_TOTAL = 4096.0
GRAD_SCALE = 2.0 * 64.0 / (2 * 256 * FRAME_TOTAL)
F32 = jnp.float32
BF16 = jnp.bfloat16
HIGHEST = lax.Precision.HIGHEST
ROWS = 104
PAY = 72


def iota(shape, axis):
    return lax.broadcasted_iota(jnp.int32, shape, axis)


def dot_f32(a, b):
    return jnp.dot(a, b, precision=HIGHEST, preferred_element_type=F32)


def tile4(x):
    return jnp.concatenate([x, x, x, x], axis=0)


def diagonal_blocks(x):
    rows, lanes = iota((128, 128), 0), iota((128, 128), 1)
    return jnp.where(rows // 32 == lanes // 32, tile4(x), 0.0)


def fold4(x):
    return (x[0:32] + x[32:64]) + (x[64:96] + x[96:128])


def unpack_blocks(packed):
    rows, lanes = iota((128, 128), 0) % 32, iota((128, 128), 1) % 32
    blocks = diagonal_blocks(packed)
    turned = blocks.T
    real = jnp.where(rows <= lanes, blocks, turned)
    imag = jnp.where(rows > lanes, blocks, jnp.where(rows < lanes, -turned, 0.0))
    return real, imag


def complex_right(real, imag):
    return jnp.concatenate(
        [jnp.concatenate([real, imag], axis=1), jnp.concatenate([-imag, real], axis=1)], axis=0
    )


def inverse(a_r, a_i):
    lane = iota((32, 128), 1)
    row = iota((32, 128), 0)
    base = (lane // 32) * 32
    col = lane % 32
    for k in range(32):
        index = base + k
        c_r = jnp.take_along_axis(a_r, index, axis=1)
        c_i = jnp.take_along_axis(a_i, index, axis=1)
        scale = 1.0 / c_r[k : k + 1, :]
        here = col[0:1] == k
        r_r = jnp.where(here, 1.0, a_r[k : k + 1, :]) * scale
        r_i = jnp.where(here, 0.0, a_i[k : k + 1, :]) * scale
        at_col = col == k
        n_r = jnp.where(at_col, 0.0, a_r) - (c_r * r_r - c_i * r_i)
        n_i = jnp.where(at_col, 0.0, a_i) - (c_r * r_i + c_i * r_r)
        at_row = row == k
        a_r = jnp.where(at_row, r_r, n_r)
        a_i = jnp.where(at_row, r_i, n_i)
    return a_r, a_i


def solve(total, pick):
    lane = iota((32, 128), 1)
    row = iota((32, 128), 0)
    eye = jnp.where(row == lane % 32, 1.0, 0.0)
    inv_t = 1.0 / FRAME_TOTAL
    s_r, s_i = [fold4(x) for x in unpack_blocks(total[0:32])]
    n_r, n_i = [fold4(x) for x in unpack_blocks(total[32:64])]
    cb_r, cb_i = unpack_blocks(total[64:96])
    d_r, d_i = total[96:97], total[97:98]
    s_r = s_r * inv_t + LOAD * eye
    s_i = s_i * inv_t
    m_r, m_i = inverse(n_r * inv_t + LOAD * eye, n_i * inv_t)
    right_m = complex_right(diagonal_blocks(m_r), diagonal_blocks(m_i))
    xh = dot_f32(jnp.concatenate([s_r, s_i], axis=1), right_m)
    xh_r, xh_i = xh[:, :128], xh[:, 128:]
    at_ref = row == pick
    conj_c_r = jnp.sum(jnp.where(at_ref, xh_r, 0.0), axis=0, keepdims=True)
    conj_c_i = jnp.sum(jnp.where(at_ref, xh_i, 0.0), axis=0, keepdims=True)
    sref_r = jnp.sum(jnp.where(at_ref, s_r, 0.0), axis=0, keepdims=True)
    sref_i = jnp.sum(jnp.where(at_ref, s_i, 0.0), axis=0, keepdims=True)
    ones = jnp.where(iota((128, 128), 0) // 32 == iota((128, 128), 1) // 32, 1.0, 0.0)
    diag = jnp.sum(xh_r * eye, axis=0, keepdims=True)
    first = dot_f32(
        jnp.concatenate(
            [
                jnp.broadcast_to(diag, (8, 128)),
                m_r * sref_r + m_i * sref_i,
                m_i * sref_r - m_r * sref_i,
            ],
            axis=0,
        ),
        ones,
    )
    inv_tau = 1.0 / first[0:1]
    c_r, c_i = first[8:40], first[40:72]
    w_r = conj_c_r * inv_tau
    w_i = -conj_c_i * inv_tau
    right_c = complex_right(cb_r, -cb_i)
    row8 = jnp.broadcast_to(jnp.concatenate([w_r, w_i], axis=1), (8, 256))
    cw = dot_f32(row8, right_c)
    g_r = GRAD_SCALE * (cw[0:1, :128] - d_r)
    g_i = GRAD_SCALE * (cw[0:1, 128:] - d_i)
    gc_r, gc_i = g_r * inv_tau, g_i * inv_tau
    gw = (g_r * w_r + g_i * w_i) * inv_tau
    second = dot_f32(
        jnp.concatenate(
            [
                jnp.broadcast_to(gw, (8, 128)),
                m_r * gc_r - m_i * gc_i,
                m_r * gc_i + m_i * gc_r,
            ],
            axis=0,
        ),
        ones,
    )
    gt2 = -2.0 * second[0:1]
    u_r, u_i = second[8:40], second[40:72]
    right_xh = complex_right(diagonal_blocks(xh_r), diagonal_blocks(xh_i))
    q = dot_f32(jnp.concatenate([m_r, m_i], axis=1), right_xh)
    uh8 = jnp.broadcast_to(jnp.concatenate([gc_r, -gc_i], axis=1), (8, 256))
    uh = dot_f32(uh8, right_m)
    uh_r, uh_i = uh[0:1, :128], uh[0:1, 128:]
    col_ref = (lane % 32) == pick
    p_r = jnp.where(col_ref, u_r, 0.0) + jnp.where(at_ref, uh_r, 0.0) + gt2 * m_r
    p_i = jnp.where(col_ref, u_i, 0.0) + jnp.where(at_ref, uh_i, 0.0) + gt2 * m_i
    n_r = (u_r * conj_c_r - u_i * conj_c_i) + (c_r * uh_r - c_i * uh_i) + gt2 * q[:, :128]
    n_i = (u_r * conj_c_i + u_i * conj_c_r) + (c_r * uh_i + c_i * uh_r) + gt2 * q[:, 128:]
    upper = row <= lane % 32
    speech = jnp.where(upper, p_r, p_i) * inv_t
    noise = jnp.where(upper, n_r, n_i) * (-inv_t)
    return speech, noise, w_r, w_i


def block_filters(filters):
    lane = iota((32, 256), 1)
    spread = jnp.where(iota((32, 256), 0) == (lane // 128) * 16 + lane % 16, 1.0, 0.0)
    wide = jnp.dot(filters, spread.astype(BF16), preferred_element_type=F32).astype(BF16)
    repeat = jnp.where(iota((512, 64), 0) // 8 == iota((512, 64), 1), 1.0, 0.0).astype(BF16)
    full = jnp.dot(repeat, wide, preferred_element_type=F32)
    keep = iota((512, 256), 0) % 8 == (iota((512, 256), 1) % 128) // 16
    return jnp.where(keep, full, 0.0).astype(BF16)


def split(x):
    high = x.astype(BF16).astype(F32)
    return high, x - high


def nt_dot(a, b):
    return lax.dot_general(a, b, (((1,), (1,)), ((), ())), preferred_element_type=F32)


def body(
    wave_ref, head_ref, filt_ref, smask_ref, nmask_ref, target_ref, pick_ref,
    enh_ref, grad_ref,
    gath, heads, frames, zz, lhs, sb, rb, pay, sgq, fg, tt, ms, mn, fb, ua,
    g_send, g_recv, h_send, h_recv, s_send, s_recv, p_send, p_recv, f_send, f_recv,
):
    d = lax.axis_index("dp")
    mu = lax.axis_index("mic")
    prev = lax.rem(d + DP - 1, DP)
    nxt = lax.rem(d + 1, DP)

    def other_d(j):
        return lax.rem(d + j, DP)

    def other_m(j):
        return lax.rem(mu + j, MIC)

    def remote(src, dst, send, recv, dev_d, dev_m):
        return pltpu.make_async_remote_copy(
            src_ref=src, dst_ref=dst, send_sem=send, recv_sem=recv,
            device_id={"dp": dev_d, "mic": dev_m}, device_id_type=pl.DeviceIdType.MESH,
        )

    barrier = pltpu.get_barrier_semaphore()

    def greet(dev_d, dev_m):
        pl.semaphore_signal(
            barrier, inc=1, device_id={"dp": dev_d, "mic": dev_m},
            device_id_type=pl.DeviceIdType.MESH,
        )

    for j in range(1, MIC):
        greet(d, other_m(j))
        greet(prev, other_m(j))
        greet(nxt, other_m(j))
    for j in range(1, DP):
        greet(other_d(j), mu)

    fb[...] = block_filters(filt_ref[...])
    ms[...] = smask_ref[...].reshape(64, TD).astype(F32)
    mn[...] = nmask_ref[...].reshape(64, TD).astype(F32)

    pl.semaphore_wait(barrier, 3 * (MIC - 1) + DP - 1)

    def wave_copy(j):
        return remote(wave_ref, gath.at[mu], g_send.at[j], g_recv.at[mu], d, other_m(j))

    def head_copy(j):
        return remote(head_ref, heads.at[mu], h_send.at[j], h_recv.at[mu], prev, other_m(j))

    for j in range(1, MIC):
        wave_copy(j).start()
    for j in range(MIC):
        head_copy(j).start()
    gath[mu] = wave_ref[...]
    for j in range(1, MIC):
        src = other_m(j)
        remote(wave_ref, gath.at[src], g_send.at[j], g_recv.at[src], d, src).wait_recv()
    for j in range(MIC):
        src = other_m(j)
        remote(head_ref, heads.at[src], h_send.at[j], h_recv.at[src], prev, src).wait_recv()

    last = d == DP - 1
    eye128 = iota((128, 128), 0) == iota((128, 128), 1)
    low = iota((1, 128), 1) < 64
    end = iota((128, TD), 1) == TD - 1
    for b in range(2):
        for q in range(4):
            x = jnp.concatenate([gath[2 * q, b], gath[2 * q + 1, b]], axis=0).astype(F32)
            head = jnp.where(low, heads[2 * q, b : b + 1, :], heads[2 * q + 1, b : b + 1, :])
            head = jnp.where(last, 0.0, head)
            column = jnp.sum(jnp.where(eye128, head, 0.0), axis=1, keepdims=True)
            moved = jnp.where(end, column, pltpu.roll(x, TD - 1, axis=1))
            frames[b, q, 0:128, :] = x.astype(BF16)
            frames[b, q, 128:256, :] = moved.astype(BF16)

    @pl.loop(0, 4)
    def _(step):
        b = step // 2
        half = step % 2
        a0 = jnp.dot(fb[...], frames[b, 2 * half], preferred_element_type=F32)
        a1 = jnp.dot(fb[...], frames[b, 2 * half + 1], preferred_element_type=F32)
        a0 = a0.reshape(8, 4, 2, 8, TD)
        a1 = a1.reshape(8, 4, 2, 8, TD)
        z = jnp.concatenate([a0, a1], axis=3).astype(BF16)
        rows = pl.ds(pl.multiple_of(16 * half, 16), 16)
        groups = pl.ds(pl.multiple_of(8 * b, 8), 8)
        zz[groups, 0, :, rows, 0:TD] = z[:, :, 0]
        zz[groups, 0, :, rows, TD : 2 * TD] = z[:, :, 1]
        zz[groups, 1, :, rows, 0:TD] = z[:, :, 1]
        zz[groups, 1, :, rows, TD : 2 * TD] = -z[:, :, 0]

    lane32 = iota((32, 128), 1)
    row32 = iota((32, 128), 0)
    upper = row32 <= lane32 % 32
    row8 = iota((8, 128), 0)
    lane8 = iota((8, 128), 1)
    own8 = row8 == lane8 // 32

    def sum_copy(j, o):
        return remote(sb.at[o], rb.at[d], s_send.at[j], s_recv.at[d], o, mu)

    def mask_row(ref, s):
        row = ref[pl.ds(s, 1), :]
        return jnp.concatenate([row, row], axis=1)

    def group_sums(o):
        b = o // 8
        f0 = (o % 8) * 4
        for g in range(4):
            tt[o, g : g + 1, 0:TD] = target_ref[b, 0, pl.ds(f0 + g, 1), :]
            tt[o, g : g + 1, TD : 2 * TD] = target_ref[b, 1, pl.ds(f0 + g, 1), :]
        tt[o, 4:8, :] = jnp.zeros((4, 2 * TD), F32)
        t = tt[o]
        turned = jnp.concatenate([-t[:, TD:], t[:, :TD]], axis=1)
        t_hi, t_lo = split(t)
        u_hi, u_lo = split(turned)
        lhs[768:800, :] = jnp.concatenate([t_hi, u_hi, t_lo, u_lo], axis=0).astype(BF16)
        for g in range(4):
            z = zz[o, 0, g].astype(F32)
            r = zz[o, 1, g].astype(F32)
            m = mask_row(ms, 4 * o + g)
            n = mask_row(mn, 4 * o + g)
            base = 192 * g
            lhs[base : base + 32, :] = (z * m).astype(BF16)
            lhs[base + 32 : base + 64, :] = (r * m).astype(BF16)
            lhs[base + 64 : base + 96, :] = (z * n).astype(BF16)
            lhs[base + 96 : base + 128, :] = (r * n).astype(BF16)
            lhs[base + 128 : base + 160, :] = z.astype(BF16)
            lhs[base + 160 : base + 192, :] = r.astype(BF16)
        right = zz[o, 0].reshape(128, 2 * TD)
        out = nt_dot(lhs[...], right)
        for kind in range(3):
            value = jnp.zeros((32, 128), F32)
            for g in range(4):
                base = 192 * g + 64 * kind
                one = jnp.where(upper, out[base : base + 32], out[base + 32 : base + 64])
                value = jnp.where(lane32 // 32 == g, one, value)
            sb[o, 32 * kind : 32 * kind + 32, :] = value
        d_r = jnp.sum(jnp.where(own8, out[768:776] + out[784:792], 0.0), axis=0, keepdims=True)
        d_i = jnp.sum(jnp.where(own8, out[776:784] + out[792:800], 0.0), axis=0, keepdims=True)
        sb[o, 96:104, :] = jnp.where(row8 == 0, d_r, jnp.where(row8 == 1, d_i, 0.0))

    @pl.loop(1, DP)
    def _(j):
        o = other_d(j)
        group_sums(o)
        sum_copy(j, o).start()

    group_sums(d)
    rb[d] = sb[d]
    for j in range(1, DP):
        src = other_d(j)
        remote(sb.at[d], rb.at[src], s_send.at[j], s_recv.at[src], src, mu).wait_recv()
    total = rb[0]
    for j in range(1, DP):
        total = total + rb[j]
    pick = jnp.where(d < DP // 2, pick_ref[0], pick_ref[1])
    speech, noise, w_r, w_i = solve(total, pick)
    pay[d, 0:32, :] = speech
    pay[d, 32:64, :] = noise
    pay[d, 64:72, :] = jnp.where(row8 == 0, w_r, jnp.where(row8 == 1, w_i, 0.0))

    def pay_copy(j):
        o = other_d(j)
        return remote(pay.at[d], pay.at[d], p_send.at[j], p_recv.at[d], o, mu)

    for j in range(1, DP):
        pay_copy(j).start()

    def group_grads(o):
        b = o // 8
        f0 = (o % 8) * 4
        right = zz[o].reshape(256, 2 * TD)
        w_r = jnp.where(own8, pay[o, 64:65, :], 0.0)
        w_i = jnp.where(own8, pay[o, 65:66, :], 0.0)
        wr_hi, wr_lo = split(w_r)
        wi_hi, wi_lo = split(w_i)
        left = jnp.concatenate(
            [jnp.concatenate([wr_hi, wi_hi], axis=1), jnp.concatenate([wr_lo, wi_lo], axis=1)],
            axis=0,
        ).astype(BF16)
        both = jnp.dot(left, right, preferred_element_type=F32)
        enh = both[0:8] + both[8:16]
        for g in range(4):
            enh_ref[b, 0, pl.ds(f0 + g, 1), :] = enh[g : g + 1, 0:TD]
            enh_ref[b, 1, pl.ds(f0 + g, 1), :] = enh[g : g + 1, TD : 2 * TD]
        e = GRAD_SCALE * (enh - tt[o])
        turned = jnp.concatenate([-e[:, TD:], e[:, :TD]], axis=1)
        e_hi, e_lo = split(e)
        r_hi, r_lo = split(turned)
        e_rows = jnp.concatenate([e_hi, r_hi, e_hi, r_hi, e_lo, r_lo], axis=0).astype(BF16)
        w_rows = jnp.concatenate([wr_hi, wi_hi, wr_lo, wi_lo, wr_hi, wi_hi], axis=0)
        direct = jnp.dot(w_rows.T.astype(BF16), e_rows, preferred_element_type=F32)
        ua[0:128, :] = direct
        s_r, s_i = unpack_blocks(pay[o, 0:32, :])
        n_r, n_i = unpack_blocks(pay[o, 32:64, :])
        mats = jnp.concatenate(
            [jnp.concatenate([s_r, -s_i], axis=1), jnp.concatenate([n_r, -n_i], axis=1)], axis=0
        )
        m_hi, m_lo = split(mats)
        applied = jnp.dot(m_hi.astype(BF16), right, preferred_element_type=F32)
        applied = applied + jnp.dot(m_lo.astype(BF16), right, preferred_element_type=F32)
        ua[128:384, :] = applied
        for g in range(4):
            at = 32 * g
            m = mask_row(ms, 4 * o + g)
            n = mask_row(mn, 4 * o + g)
            sg = (
                ua[at : at + 32, :]
                + m * ua[128 + at : 160 + at, :]
                + n * ua[256 + at : 288 + at, :]
            )
            place = pl.ds(pl.multiple_of(16 * (f0 + g), 16), 16)
            for q in range(4):
                piece = sg[8 * q : 8 * q + 8]
                sgq[b, q, place, :] = jnp.concatenate(
                    [piece[:, :TD], piece[:, TD:]], axis=0
                ).astype(BF16)

    group_grads(d)

    @pl.loop(1, DP)
    def _(j):
        o = other_d(j)
        remote(pay.at[d], pay.at[o], p_send.at[j], p_recv.at[o], o, mu).wait_recv()
        group_grads(o)

    acc = jnp.zeros((512, 256), F32)
    for b in range(2):
        for q in range(4):
            acc = acc + nt_dot(sgq[b, q], frames[b, q])
    keep = iota((512, 256), 0) % 8 == (iota((512, 256), 1) % 128) // 16
    rows = jnp.sum(jnp.where(keep, acc, 0.0).reshape(64, 8, 256), axis=1)
    at, lane = iota((256, 128), 0), iota((256, 128), 1)
    tap = (at // 128) * 16 + at % 16
    part = jnp.zeros((16, 128), F32)
    for p in range(4):
        place = jnp.where((lane // 32 == p) & (lane % 32 == tap), 1.0, 0.0)
        part = part + dot_f32(rows[16 * p : 16 * p + 16], place)
    fg[d] = part

    def grad_copy(j):
        return remote(fg.at[d], fg.at[d], f_send.at[j], f_recv.at[d], other_d(j), mu)

    for j in range(1, DP):
        grad_copy(j).start()
    for j in range(1, DP):
        src = other_d(j)
        remote(fg.at[d], fg.at[src], f_send.at[j], f_recv.at[src], src, mu).wait_recv()
    result = fg[0]
    for j in range(1, DP):
        result = result + fg[j]
    grad_ref[...] = result

    for j in range(1, MIC):
        wave_copy(j).wait_send()
    for j in range(MIC):
        head_copy(j).wait_send()
    for j in range(1, DP):
        sum_copy(j, other_d(j)).wait_send()
        pay_copy(j).wait_send()
        grad_copy(j).wait_send()


def local(waveform, filters, speech_mask, noise_mask, target, ref_mic):
    wave = waveform.reshape(2, 4, TD, 16).transpose(0, 1, 3, 2).reshape(2, 64, TD)
    head = waveform[:, :, :16].reshape(2, 64).astype(F32)
    head = jnp.pad(jnp.concatenate([head, head], axis=1), ((0, 6), (0, 0)))
    vmem = pl.BlockSpec(memory_space=pltpu.VMEM)
    dma = pltpu.SemaphoreType.DMA
    enhanced, grad = pl.pallas_call(
        body,
        out_shape=(
            jax.ShapeDtypeStruct((2, 2, 32, TD), F32),
            jax.ShapeDtypeStruct((16, 128), F32),
        ),
        in_specs=[vmem] * 6 + [pl.BlockSpec(memory_space=pltpu.SMEM)],
        out_specs=(vmem, vmem),
        scratch_shapes=[
            pltpu.VMEM((MIC, 2, 64, TD), BF16),
            pltpu.VMEM((MIC, 8, 128), F32),
            pltpu.VMEM((2, 4, 256, TD), BF16),
            pltpu.VMEM((16, 2, 4, 32, 2 * TD), BF16),
            pltpu.VMEM((800, 2 * TD), BF16),
            pltpu.VMEM((DP, ROWS, 128), F32),
            pltpu.VMEM((DP, ROWS, 128), F32),
            pltpu.VMEM((DP, PAY, 128), F32),
            pltpu.VMEM((2, 4, 512, TD), BF16),
            pltpu.VMEM((DP, 16, 128), F32),
            pltpu.VMEM((DP, 8, 2 * TD), F32),
            pltpu.VMEM((64, TD), F32),
            pltpu.VMEM((64, TD), F32),
            pltpu.VMEM((512, 256), BF16),
            pltpu.VMEM((384, 2 * TD), F32),
            dma((MIC,)), dma((MIC,)), dma((MIC,)), dma((MIC,)),
            dma((DP,)), dma((DP,)), dma((DP,)), dma((DP,)), dma((DP,)), dma((DP,)),
        ],
        compiler_params=pltpu.CompilerParams(
            collective_id=0, has_side_effects=True, vmem_limit_bytes=60 * 1024 * 1024
        ),
    )(wave, head, filters, speech_mask, noise_mask, target, ref_mic)
    filter_grad = grad.reshape(16, 4, 32).transpose(1, 0, 2).reshape(64, 32)
    return (enhanced, filter_grad)


def solution(mesh):
    in_specs = (
        P(None, "mic", "dp"),
        P("mic", None),
        P(None, "mic", "dp"),
        P(None, "mic", "dp"),
        P(None, None, "mic", "dp"),
        P(),
    )
    out_specs = (P(None, None, "mic", "dp"), P("mic", None))
    return jax.shard_map(local, mesh=mesh, in_specs=in_specs, out_specs=out_specs, check_vma=False)
```

time: 1270 us -> 68.7 us (0.05)
  other arithmetic: 687 us -> 0.66 us
  waiting for transfers between devices: 207 us -> 0 us
  blocking collectives: 192 us -> 0 us
  local copies, waits for them, and re-layouts: 86.6 us -> 5.68 us
  matrix products: 75.4 us -> 0 us
  Pallas kernels: 0 us -> 61.4 us
  between operations: 14.8 us -> 0.67 us
    another operation x11 -> x0, other arithmetic: 657 us -> none  [the longest x6 517 us: beam_weights(): factor = jnp.linalg.cholesky(noise_cov)]
    psum x1 -> x0, waiting for transfers between devices: 137 us -> none  [local(): summed = lax.psum(statistics, 'dp')]
    psum x2 -> x0, blocking collectives: 106 us -> none  [the longest x1 54.6 us: local(): beam_grad = lax.psum(beam_part, 'dp')]
    unnamed x3 -> x0, waiting for transfers between devices: 69.7 us -> none
    pallas_call x0 -> x1, Pallas kernels: none -> 61.4 us  [local(): pl.pallas_call(body, out_shape=(jax.ShapeDtypeStruct((2, 2, 32, TD), F32)...]
    all_to_all x2 -> x0, blocking collectives: 55.9 us -> none  [the longest x1 28.8 us: local(): lax.all_to_all(shaped_grad, 'mic', split_axis=3, concat_axis=1, tiled=True)]
    dot_general x15 -> x0, matrix products: 50 us -> none  [the longest x1 6.82 us: local(): jnp.einsum('bfij,bfjt->bfit', noise_grad, stacked_wide, precision=highest)]
    all_gather x1 -> x0, blocking collectives: 29.2 us -> none  [local(): every_filter = lax.all_gather(filters, 'mic', axis=0, tiled=True)]
  transfers between devices with their start and end apart: 3 -> 0, of which waited for: 2 -> 0; matrix products, arithmetic and copies ran while one was open for 0% -> 0% of each run, Pallas kernels for 0% -> 0%
where the time goes in v1:
time: 68.7 us; the launch traced here: 68.5 us
  Pallas kernels  61.4 us (89%)
  local copies, waits for them, and re-layouts  5.68 us (8%)
    pallas_call x1, Pallas kernels, local(): pl.pallas_call(body, out_shape=(jax.ShapeDtypeStruct((2, 2, 32, TD), F32)...  61.4 us
    unnamed x7, local copies, waits for them, and re-layouts  2.04 us

profile of v1, /device:TPU:1, one launch (start us, length us, event | category | flops | bytes accessed | tf_op | source)
XLA Modules:
  0.0 68.5 jit_solution(13784922320555852297)
XLA Ops:
  0.6 1.2 %reshape.19 = bf16[2,4,256,16]{3,2,1,0:T(8,128)(2,1)S(1)} reshape(bf16[2,4,4096]{2,1,0:T(4,128)(2,1)} %param.6) | data formatting | bytes 131072 | tf_op jit(solution)/shard_map/reshape | solution.py:438
  1.9 0.0 copy-start.1
  1.9 0.8 %copy.11 = bf16[2,4,16,256]{3,2,1,0:T(8,128)(2,1)} copy(bf16[2,4,16,256]{2,3,1,0:T(8,128)(2,1)S(1)} %bitcast.5) | data formatting | bytes 131072 | tf_op jit(solution)/shard_map/transpose | solution.py:438
  2.7 0.0 copy-done.1
  2.7 0.7 %copy.12.filt_ref = bf16[64,32]{1,0:T(8,128)(2,1)} copy(bf16[64,32]{0,1:T(8,128)(2,1)S(1)} %copy-done.1) | data formatting | bytes 8192 | tf_op args[1]
  3.4 0.0 slice-start
  3.4 0.7 slice-done
  4.1 0.1 convert_element_type.6
  4.2 0.7 fusion.3.head_ref
  4.8 61.4 %shard_map.77 = (f32[2,2,32,256]{3,2,1,0:T(8,128)}, f32[16,128]{1,0:T(8,128)}) custom-call(bf16[2,64,256]{2,1,0:T(8,128)(2,1)} %bitcast.6, f32[8,128]{1,0:T(8,128)} %fusion.3.head_ref, bf16[64,32]{1,0:T(8,128)(2,1)} %copy.12.filt_ref, bf16[2,32,256]{2,1,0:T(8,128)(2,1)} %smask_ref.1, bf16[2,32,256]{2,1,0:T(8,128)(2,1)} %nmask_ref.1, ...), custom_call_target="tpu_custom_call" | custom-call | tf_op jit(solution)/shard_map/pallas_call | solution.py:443
  66.3 0.0 copy-start
  66.3 0.8 %reshape.21 = f32[16,4,32]{2,1,0:T(4,128)S(1)} reshape(f32[16,128]{1,0:T(8,128)} %get-tuple-element.5) | data formatting | bytes 16384 | tf_op jit(solution)/shard_map/reshape | solution.py:474
  67.1 0.7 copy.14
  67.8 0.0 copy-done
  67.8 0.7 copy.16
  (1 shorter events, 0.0 us)
Async XLA Ops:
  1.9 0.8 %copy-start.1 = (bf16[64,32]{0,1:T(8,128)(2,1)S(1)}, bf16[64,32]{0,1:T(8,128)(2,1)}, u32[]{:S(2)}) copy-start(bf16[64,32]{0,1:T(8,128)(2,1)} %param.7) | copy-start | bytes 12292
  3.4 0.7 slice-start
  66.3 1.5 %copy-start = (f32[2,2,32,256]{3,2,1,0:T(8,128)S(1)}, f32[2,2,32,256]{3,2,1,0:T(8,128)}, u32[]{:S(2)}) copy-start(f32[2,2,32,256]{3,2,1,0:T(8,128)} %get-tuple-element.10) | copy-start | bytes 393220

commit v2 on v1

--- a/solution.py
+++ b/solution.py
@@ -179,6 +179,18 @@
     mu = lax.axis_index("mic")
     prev = lax.rem(d + DP - 1, DP)
     nxt = lax.rem(d + 1, DP)
+    at_z, at_x, at_c = d // 4, (d // 2) % 2, d % 2
+
+    def rel(dz, dx, dc):
+        return ((at_z + dz) % 4) * 4 + ((at_x + dx) % 2) * 2 + (at_c + dc) % 2
+
+    def table(i, values):
+        out = values[0]
+        for k in range(1, len(values)):
+            out = jnp.where(i == k, values[k], out)
+        return out
+
+    core, side, up, down = rel(0, 0, 1), rel(0, 1, 0), rel(1, 0, 0), rel(3, 0, 0)
 
     def other_d(j):
         return lax.rem(d + j, DP)
@@ -202,34 +214,37 @@
 
     for j in range(1, MIC):
         greet(d, other_m(j))
-        greet(prev, other_m(j))
-        greet(nxt, other_m(j))
-    for j in range(1, DP):
-        greet(other_d(j), mu)
+    for peer in (core, side, up, down, prev, nxt):
+        greet(peer, mu)
 
     fb[...] = block_filters(filt_ref[...])
     ms[...] = smask_ref[...].reshape(64, TD).astype(F32)
     mn[...] = nmask_ref[...].reshape(64, TD).astype(F32)
 
-    pl.semaphore_wait(barrier, 3 * (MIC - 1) + DP - 1)
+    pl.semaphore_wait(barrier, MIC + 5)
 
     def wave_copy(j):
         return remote(wave_ref, gath.at[mu], g_send.at[j], g_recv.at[mu], d, other_m(j))
 
     def head_copy(j):
-        return remote(head_ref, heads.at[mu], h_send.at[j], h_recv.at[mu], prev, other_m(j))
-
+        return remote(heads.at[mu], heads.at[mu], h_send.at[j], h_recv.at[mu], d, other_m(j))
+
+    def head_first():
+        return remote(head_ref, heads.at[mu], h_send.at[0], h_recv.at[mu], prev, mu)
+
+    head_first().start()
     for j in range(1, MIC):
         wave_copy(j).start()
-    for j in range(MIC):
+    gath[mu] = wave_ref[...]
+    head_first().wait_recv()
+    for j in range(1, MIC):
         head_copy(j).start()
-    gath[mu] = wave_ref[...]
     for j in range(1, MIC):
         src = other_m(j)
         remote(wave_ref, gath.at[src], g_send.at[j], g_recv.at[src], d, src).wait_recv()
-    for j in range(MIC):
+    for j in range(1, MIC):
         src = other_m(j)
-        remote(head_ref, heads.at[src], h_send.at[j], h_recv.at[src], prev, src).wait_recv()
+        remote(heads.at[mu], heads.at[src], h_send.at[j], h_recv.at[src], d, src).wait_recv()
 
     last = d == DP - 1
     eye128 = iota((128, 128), 0) == iota((128, 128), 1)
@@ -267,9 +282,6 @@
     row8 = iota((8, 128), 0)
     lane8 = iota((8, 128), 1)
     own8 = row8 == lane8 // 32
-
-    def sum_copy(j, o):
-        return remote(sb.at[o], rb.at[d], s_send.at[j], s_recv.at[d], o, mu)
 
     def mask_row(ref, s):
         row = ref[pl.ds(s, 1), :]
@@ -312,32 +324,78 @@
         d_i = jnp.sum(jnp.where(own8, out[776:784] + out[792:800], 0.0), axis=0, keepdims=True)
         sb[o, 96:104, :] = jnp.where(row8 == 0, d_r, jnp.where(row8 == 1, d_i, 0.0))
 
-    @pl.loop(1, DP)
-    def _(j):
-        o = other_d(j)
+    def sum_copy(o, slot, sem, dev):
+        return remote(sb.at[o], rb.at[slot], s_send.at[sem], s_recv.at[slot], dev, mu)
+
+    def add_slot(o, slot):
+        sum_copy(o, slot, slot, core).wait_recv()
+        sb[o] = sb[o] + rb[slot]
+
+    order = [(2, 0, 1), (2, 1, 1), (2, 0, 0), (2, 1, 0), (3, 0, 1), (1, 1, 1), (1, 0, 1), (3, 1, 1),
+             (3, 0, 0), (1, 1, 0), (1, 0, 0), (3, 1, 0), (0, 1, 1), (0, 0, 1), (0, 1, 0), (0, 0, 0)]
+
+    @pl.loop(0, DP)
+    def _(i):
+        dz = table(i, [k[0] for k in order])
+        dx = table(i, [k[1] for k in order])
+        dc = table(i, [k[2] for k in order])
+        o = rel(dz, dx, dc)
+        slot = o // 2
         group_sums(o)
-        sum_copy(j, o).start()
-
-    group_sums(d)
-    rb[d] = sb[d]
-    for j in range(1, DP):
-        src = other_d(j)
-        remote(sb.at[d], rb.at[src], s_send.at[j], s_recv.at[src], src, mu).wait_recv()
-    total = rb[0]
-    for j in range(1, DP):
-        total = total + rb[j]
+
+        @pl.when(dc == 1)
+        def _():
+            sum_copy(o, slot, slot, core).start()
+
+        @pl.when(dc == 0)
+        def _():
+            add_slot(o, slot)
+
+        @pl.when(i == 2)
+        def _():
+            sum_copy(o, 8, 8, up).start()
+
+        @pl.when(i == 3)
+        def _():
+            sum_copy(o, 9, 9, down).start()
+
+        @pl.when(i == 8)
+        def _():
+            sum_copy(o, 12, 10, down).start()
+
+        @pl.when(i == 9)
+        def _():
+            sum_copy(o, 13, 11, up).start()
+
+        @pl.when(i == 10)
+        def _():
+            add_slot(o, 8)
+            sum_copy(o, 10, 12, up).start()
+
+        @pl.when(i == 11)
+        def _():
+            add_slot(o, 9)
+            sum_copy(o, 11, 13, down).start()
+
+    across = rel(0, 1, 0)
+    add_slot(across, 13)
+    add_slot(across, 11)
+    sum_copy(across, 14, 14, side).start()
+    add_slot(d, 12)
+    add_slot(d, 10)
+    add_slot(d, 14)
+    total = sb[d]
     pick = jnp.where(d < DP // 2, pick_ref[0], pick_ref[1])
     speech, noise, w_r, w_i = solve(total, pick)
     pay[d, 0:32, :] = speech
     pay[d, 32:64, :] = noise
     pay[d, 64:72, :] = jnp.where(row8 == 0, w_r, jnp.where(row8 == 1, w_i, 0.0))
 
-    def pay_copy(j):
-        o = other_d(j)
-        return remote(pay.at[d], pay.at[d], p_send.at[j], p_recv.at[d], o, mu)
-
-    for j in range(1, DP):
-        pay_copy(j).start()
+    def pay_copy(o, sem, dev):
+        return remote(pay.at[o], pay.at[o], p_send.at[sem], p_recv.at[o], dev, mu)
+
+    for k, dev in enumerate((side, up, down, core)):
+        pay_copy(d, k, dev).start()
 
     def group_grads(o):
         b = o // 8
@@ -389,12 +447,37 @@
                     [piece[:, :TD], piece[:, TD:]], axis=0
                 ).astype(BF16)
 
-    group_grads(d)
-
-    @pl.loop(1, DP)
-    def _(j):
-        o = other_d(j)
-        remote(pay.at[d], pay.at[o], p_send.at[j], p_recv.at[o], o, mu).wait_recv()
+    spread = [(0, 0, 0), (0, 0, 1), (0, 1, 0), (3, 0, 0), (1, 0, 0), (3, 1, 0), (1, 1, 0), (2, 0, 0),
+              (2, 1, 0), (0, 1, 1), (3, 0, 1), (1, 0, 1), (3, 1, 1), (1, 1, 1), (2, 0, 1), (2, 1, 1)]
+
+    @pl.loop(0, DP)
+    def _(i):
+        dz = table(i, [k[0] for k in spread])
+        dx = table(i, [k[1] for k in spread])
+        dc = table(i, [k[2] for k in spread])
+        o = rel(dz, dx, dc)
+
+        @pl.when(i > 0)
+        def _():
+            pay_copy(o, 0, core).wait_recv()
+
+        @pl.when(i == 2)
+        def _():
+            pay_copy(o, 4, up).start()
+            pay_copy(o, 5, down).start()
+
+        @pl.when(i == 3)
+        def _():
+            pay_copy(o, 6, up).start()
+
+        @pl.when(i == 6)
+        def _():
+            pay_copy(o, 7, down).start()
+
+        @pl.when((i >= 2) & (i <= 8))
+        def _():
+            pay_copy(o, 6 + i, core).start()
+
         group_grads(o)
 
     acc = jnp.zeros((512, 256), F32)
@@ -424,13 +507,14 @@
         result = result + fg[j]
     grad_ref[...] = result
 
+    head_first().wait_send()
     for j in range(1, MIC):
         wave_copy(j).wait_send()
-    for j in range(MIC):
         head_copy(j).wait_send()
+    for j in range(DP - 1):
+        sum_copy(d, 0, j, core).wait_send()
+        pay_copy(d, j, core).wait_send()
     for j in range(1, DP):
-        sum_copy(j, other_d(j)).wait_send()
-        pay_copy(j).wait_send()
         grad_copy(j).wait_send()
 
 
@@ -455,7 +539,7 @@
             pltpu.VMEM((16, 2, 4, 32, 2 * TD), BF16),
             pltpu.VMEM((800, 2 * TD), BF16),
             pltpu.VMEM((DP, ROWS, 128), F32),
-            pltpu.VMEM((DP, ROWS, 128), F32),
+            pltpu.VMEM((DP - 1, ROWS, 128), F32),
             pltpu.VMEM((DP, PAY, 128), F32),
             pltpu.VMEM((2, 4, 512, TD), BF16),
             pltpu.VMEM((DP, 16, 128), F32),

time: 68.7 us -> 65.9 us (0.959)
  Pallas kernels: 61.4 us -> 58.7 us
    pallas_call x1, Pallas kernels: 61.4 us -> 58.7 us  [local(): pl.pallas_call(body, out_shape=(jax.ShapeDtypeStruct((2, 2, 32, TD), F32)...]
where the time goes in v2:
time: 65.9 us; the launch traced here: 65.7 us
  Pallas kernels  58.7 us (89%)
  local copies, waits for them, and re-layouts  5.68 us (9%)
  between operations  0.67 us (1%)
  other arithmetic  0.66 us (1%)
    pallas_call x1, Pallas kernels, local(): pl.pallas_call(body, out_shape=(jax.ShapeDtypeStruct((2, 2, 32, TD), F32)...  58.7 us
    unnamed x7, local copies, waits for them, and re-layouts  2.04 us

profile of v2, /device:TPU:1, one launch (start us, length us, event | category | flops | bytes accessed | tf_op | source)
XLA Modules:
  0.0 65.7 jit_solution(12642705911215130998)
XLA Ops:
  0.6 1.2 %reshape.19 = bf16[2,4,256,16]{3,2,1,0:T(8,128)(2,1)S(1)} reshape(bf16[2,4,4096]{2,1,0:T(4,128)(2,1)} %param.6) | data formatting | bytes 131072 | tf_op jit(solution)/shard_map/reshape | solution.py:522
  1.9 0.0 copy-start.1
  1.9 0.8 %copy.11 = bf16[2,4,16,256]{3,2,1,0:T(8,128)(2,1)} copy(bf16[2,4,16,256]{2,3,1,0:T(8,128)(2,1)S(1)} %bitcast.5) | data formatting | bytes 131072 | tf_op jit(solution)/shard_map/transpose | solution.py:522
  2.7 0.0 copy-done.1
  2.7 0.7 %copy.12.filt_ref = bf16[64,32]{1,0:T(8,128)(2,1)} copy(bf16[64,32]{0,1:T(8,128)(2,1)S(1)} %copy-done.1) | data formatting | bytes 8192 | tf_op args[1]
  3.4 0.0 slice-start
  3.4 0.7 %slice-done = bf16[2,4,16]{2,1,0:T(4,128)(2,1)S(1)} async-done(((bf16[2,4,4096]{2,1,0:T(4,128)(2,1)}), bf16[2,4,16]{2,1,0:T(4,128)(2,1)S(1)}, s32[]{:S(2)}) %slice-start) | async-done | bytes 280 | tf_op jit(solution)/shard_map/slice | solution.py:523
  4.1 0.1 convert_element_type.6
  4.2 0.7 %fusion.3.head_ref = f32[8,128]{1,0:T(8,128)} fusion(bf16[2,64]{1,0:T(2,128)(2,1)S(1)} %convert_element_type.6), kind=kLoop, calls=%fused_computation.4 | loop fusion | flops 7168 | bytes 4352 | tf_op jit(solution)/shard_map/jit(_pad)/pad | solution.py:524
  4.8 58.7 %shard_map.77 = (f32[2,2,32,256]{3,2,1,0:T(8,128)}, f32[16,128]{1,0:T(8,128)}) custom-call(bf16[2,64,256]{2,1,0:T(8,128)(2,1)} %bitcast.6, f32[8,128]{1,0:T(8,128)} %fusion.3.head_ref, bf16[64,32]{1,0:T(8,128)(2,1)} %copy.12.filt_ref, bf16[2,32,256]{2,1,0:T(8,128)(2,1)} %smask_ref.1, bf16[2,32,256]{2,1,0:T(8,128)(2,1)} %nmask_ref.1, ...), custom_call_target="tpu_custom_call" | custom-call | tf_op jit(solution)/shard_map/pallas_call | solution.py:527
  63.5 0.0 copy-start
  63.5 0.8 %reshape.21 = f32[16,4,32]{2,1,0:T(4,128)S(1)} reshape(f32[16,128]{1,0:T(8,128)} %get-tuple-element.5) | data formatting | bytes 16384 | tf_op jit(solution)/shard_map/reshape | solution.py:558
  64.3 0.7 %copy.14 = f32[64,32]{0,1:T(8,128)} copy(f32[64,32]{1,0:T(8,128)S(1)} %bitcast.7) | data formatting | bytes 16384
  65.0 0.0 copy-done
  65.0 0.7 copy.16
  (1 shorter events, 0.0 us)
Async XLA Ops:
  1.9 0.8 %copy-start.1 = (bf16[64,32]{0,1:T(8,128)(2,1)S(1)}, bf16[64,32]{0,1:T(8,128)(2,1)}, u32[]{:S(2)}) copy-start(bf16[64,32]{0,1:T(8,128)(2,1)} %param.7) | copy-start | bytes 12292
  3.4 0.7 %slice-start = ((bf16[2,4,4096]{2,1,0:T(4,128)(2,1)}), bf16[2,4,16]{2,1,0:T(4,128)(2,1)S(1)}, s32[]{:S(2)}) async-start(bf16[2,4,4096]{2,1,0:T(4,128)(2,1)} %param.6), calls=%async_computation | async-start | bytes 4096 | tf_op jit(solution)/shard_map/slice | solution.py:523
  63.5 1.5 %copy-start = (f32[2,2,32,256]{3,2,1,0:T(8,128)S(1)}, f32[2,2,32,256]{3,2,1,0:T(8,128)}, u32[]{:S(2)}) copy-start(f32[2,2,32,256]{3,2,1,0:T(8,128)} %get-tuple-element.10) | copy-start | bytes 393220

commit v3 on v1

v3 whole, which is shorter than its diff:
```python
import jax
import jax.numpy as jnp
from jax import lax
from jax.experimental import pallas as pl
from jax.experimental.pallas import tpu as pltpu
from jax.sharding import PartitionSpec as P

DP = 16
MIC = 8
MICS = 32
TD = 256
LOAD = 0.05
FRAME_TOTAL = 4096.0
GRAD_SCALE = 2.0 * 64.0 / (2 * 256 * FRAME_TOTAL)
F32 = jnp.float32
BF16 = jnp.bfloat16
HIGHEST = lax.Precision.HIGHEST
ROWS = 104
PAY = 72


def iota(shape, axis):
    return lax.broadcasted_iota(jnp.int32, shape, axis)


def dot_f32(a, b):
    return jnp.dot(a, b, precision=HIGHEST, preferred_element_type=F32)


def tile4(x):
    return jnp.concatenate([x, x, x, x], axis=0)


def diagonal_blocks(x):
    rows, lanes = iota((128, 128), 0), iota((128, 128), 1)
    return jnp.where(rows // 32 == lanes // 32, tile4(x), 0.0)


def fold4(x):
    return (x[0:32] + x[32:64]) + (x[64:96] + x[96:128])


def unpack_blocks(packed):
    rows, lanes = iota((128, 128), 0) % 32, iota((128, 128), 1) % 32
    blocks = diagonal_blocks(packed)
    turned = blocks.T
    real = jnp.where(rows <= lanes, blocks, turned)
    imag = jnp.where(rows > lanes, blocks, jnp.where(rows < lanes, -turned, 0.0))
    return real, imag


def complex_right(real, imag):
    return jnp.concatenate(
        [jnp.concatenate([real, imag], axis=1), jnp.concatenate([-imag, real], axis=1)], axis=0
    )


def inverse(a_r, a_i):
    lane = iota((32, 128), 1)
    row = iota((32, 128), 0)
    base = (lane // 32) * 32
    col = lane % 32
    for k in range(32):
        index = base + k
        c_r = jnp.take_along_axis(a_r, index, axis=1)
        c_i = jnp.take_along_axis(a_i, index, axis=1)
        scale = 1.0 / c_r[k : k + 1, :]
        here = col[0:1] == k
        r_r = jnp.where(here, 1.0, a_r[k : k + 1, :]) * scale
        r_i = jnp.where(here, 0.0, a_i[k : k + 1, :]) * scale
        at_col = col == k
        n_r = jnp.where(at_col, 0.0, a_r) - (c_r * r_r - c_i * r_i)
        n_i = jnp.where(at_col, 0.0, a_i) - (c_r * r_i + c_i * r_r)
        at_row = row == k
        a_r = jnp.where(at_row, r_r, n_r)
        a_i = jnp.where(at_row, r_i, n_i)
    return a_r, a_i


def solve(total, pick):
    lane = iota((32, 128), 1)
    row = iota((32, 128), 0)
    eye = jnp.where(row == lane % 32, 1.0, 0.0)
    inv_t = 1.0 / FRAME_TOTAL
    s_r, s_i = [fold4(x) for x in unpack_blocks(total[0:32])]
    n_r, n_i = [fold4(x) for x in unpack_blocks(total[32:64])]
    cb_r, cb_i = unpack_blocks(total[64:96])
    d_r, d_i = total[96:97], total[97:98]
    s_r = s_r * inv_t + LOAD * eye
    s_i = s_i * inv_t
    m_r, m_i = inverse(n_r * inv_t + LOAD * eye, n_i * inv_t)
    right_m = complex_right(diagonal_blocks(m_r), diagonal_blocks(m_i))
    xh = dot_f32(jnp.concatenate([s_r, s_i], axis=1), right_m)
    xh_r, xh_i = xh[:, :128], xh[:, 128:]
    at_ref = row == pick
    conj_c_r = jnp.sum(jnp.where(at_ref, xh_r, 0.0), axis=0, keepdims=True)
    conj_c_i = jnp.sum(jnp.where(at_ref, xh_i, 0.0), axis=0, keepdims=True)
    sref_r = jnp.sum(jnp.where(at_ref, s_r, 0.0), axis=0, keepdims=True)
    sref_i = jnp.sum(jnp.where(at_ref, s_i, 0.0), axis=0, keepdims=True)
    ones = jnp.where(iota((128, 128), 0) // 32 == iota((128, 128), 1) // 32, 1.0, 0.0)
    diag = jnp.sum(xh_r * eye, axis=0, keepdims=True)
    first = dot_f32(
        jnp.concatenate(
            [
                jnp.broadcast_to(diag, (8, 128)),
                m_r * sref_r + m_i * sref_i,
                m_i * sref_r - m_r * sref_i,
            ],
            axis=0,
        ),
        ones,
    )
    inv_tau = 1.0 / first[0:1]
    c_r, c_i = first[8:40], first[40:72]
    w_r = conj_c_r * inv_tau
    w_i = -conj_c_i * inv_tau
    right_c = complex_right(cb_r, -cb_i)
    row8 = jnp.broadcast_to(jnp.concatenate([w_r, w_i], axis=1), (8, 256))
    cw = dot_f32(row8, right_c)
    g_r = GRAD_SCALE * (cw[0:1, :128] - d_r)
    g_i = GRAD_SCALE * (cw[0:1, 128:] - d_i)
    gc_r, gc_i = g_r * inv_tau, g_i * inv_tau
    gw = (g_r * w_r + g_i * w_i) * inv_tau
    second = dot_f32(
        jnp.concatenate(
            [
                jnp.broadcast_to(gw, (8, 128)),
                m_r * gc_r - m_i * gc_i,
                m_r * gc_i + m_i * gc_r,
            ],
            axis=0,
        ),
        ones,
    )
    gt2 = -2.0 * second[0:1]
    u_r, u_i = second[8:40], second[40:72]
    right_xh = complex_right(diagonal_blocks(xh_r), diagonal_blocks(xh_i))
    q = dot_f32(jnp.concatenate([m_r, m_i], axis=1), right_xh)
    uh8 = jnp.broadcast_to(jnp.concatenate([gc_r, -gc_i], axis=1), (8, 256))
    uh = dot_f32(uh8, right_m)
    uh_r, uh_i = uh[0:1, :128], uh[0:1, 128:]
    col_ref = (lane % 32) == pick
    p_r = jnp.where(col_ref, u_r, 0.0) + jnp.where(at_ref, uh_r, 0.0) + gt2 * m_r
    p_i = jnp.where(col_ref, u_i, 0.0) + jnp.where(at_ref, uh_i, 0.0) + gt2 * m_i
    n_r = (u_r * conj_c_r - u_i * conj_c_i) + (c_r * uh_r - c_i * uh_i) + gt2 * q[:, :128]
    n_i = (u_r * conj_c_i + u_i * conj_c_r) + (c_r * uh_i + c_i * uh_r) + gt2 * q[:, 128:]
    upper = row <= lane % 32
    speech = jnp.where(upper, p_r, p_i) * inv_t
    noise = jnp.where(upper, n_r, n_i) * (-inv_t)
    return speech, noise, w_r, w_i


def tn_dot(a, b):
    return lax.dot_general(a, b, (((0,), (0,)), ((), ())), preferred_element_type=F32)


def block_filters(filters_t):
    lane = iota((32, 256), 1)
    spread = jnp.where(iota((32, 256), 0) == (lane // 128) * 16 + lane % 16, 1.0, 0.0)
    wide = tn_dot(filters_t, spread.astype(BF16)).astype(BF16)
    repeat = jnp.where(iota((512, 64), 0) // 8 == iota((512, 64), 1), 1.0, 0.0).astype(BF16)
    full = jnp.dot(repeat, wide, preferred_element_type=F32)
    keep = iota((512, 256), 0) % 8 == (iota((512, 256), 1) % 128) // 16
    return jnp.where(keep, full, 0.0).astype(BF16)


def split(x):
    high = x.astype(BF16).astype(F32)
    return high, x - high


def nt_dot(a, b):
    return lax.dot_general(a, b, (((1,), (1,)), ((), ())), preferred_element_type=F32)


def body(
    wave_ref, filt_ref, smask_ref, nmask_ref, target_ref, pick_ref,
    enh_ref, grad_ref,
    wblk, head, gath, heads, frames, zz, yy, lhs, sb, rb, pay, sgq, fg, tt, ms, mn, fb,
    g_send, g_recv, h_send, h_recv, s_send, s_recv, p_send, p_recv, f_send, f_recv,
):
    d = lax.axis_index("dp")
    mu = lax.axis_index("mic")
    prev = lax.rem(d + DP - 1, DP)
    nxt = lax.rem(d + 1, DP)
    at_z, at_x, at_c = d // 4, (d // 2) % 2, d % 2
    chip = d // 2
    core = 2 * chip + 1 - at_c

    def rel(dz, dx, dc):
        return ((at_z + dz) % 4) * 4 + ((at_x + dx) % 2) * 2 + (at_c + dc) % 2

    others = [rel(0, 1, 0), rel(1, 0, 0), rel(3, 0, 0), rel(1, 1, 0), rel(3, 1, 0), rel(2, 0, 0), rel(2, 1, 0)]

    def table(i, values):
        out = values[0]
        for k in range(1, len(values)):
            out = jnp.where(i == k, values[k], out)
        return out

    def other_d(j):
        return lax.rem(d + j, DP)

    def other_m(j):
        return lax.rem(mu + j, MIC)

    def remote(src, dst, send, recv, dev_d, dev_m):
        return pltpu.make_async_remote_copy(
            src_ref=src, dst_ref=dst, send_sem=send, recv_sem=recv,
            device_id={"dp": dev_d, "mic": dev_m}, device_id_type=pl.DeviceIdType.MESH,
        )

    barrier = pltpu.get_barrier_semaphore()

    def greet(dev_d, dev_m):
        pl.semaphore_signal(
            barrier, inc=1, device_id={"dp": dev_d, "mic": dev_m},
            device_id_type=pl.DeviceIdType.MESH,
        )

    for j in range(1, MIC):
        greet(d, other_m(j))
    for peer in others + [core, prev, nxt]:
        greet(peer, mu)

    turn = iota((128, 1024), 0)
    lane = iota((128, 1024), 1)
    choose = (turn % 4 == lane // TD) & (turn // 4 == (lane % TD) // 8)
    choose = jnp.where(choose, 1.0, 0.0).astype(BF16)
    phase = iota((16, 1024), 1) % 8
    for b in range(2):
        rows = wave_ref[b].astype(F32)
        head[4 * b : 4 * b + 4, :] = rows[:, 0:128]
        stacked = jnp.concatenate([rows[:, 128 * r : 128 * r + 128] for r in range(32)], axis=0)
        spread = jnp.dot(stacked.T.astype(BF16), choose, preferred_element_type=F32)
        taps = spread[0:16]
        for k in range(1, 8):
            taps = jnp.where(phase == k, spread[16 * k : 16 * k + 16], taps)
        for m in range(4):
            wblk[b, 16 * m : 16 * m + 16, :] = taps[:, TD * m : TD * m + TD].astype(BF16)

    fb[...] = block_filters(filt_ref[...])
    ms[...] = smask_ref[...].reshape(64, TD).astype(F32)
    mn[...] = nmask_ref[...].reshape(64, TD).astype(F32)
    for o in range(DP):
        for v in range(2):
            tt[o, 8 * v : 8 * v + 4, :] = target_ref[o // 8, v, (o % 8) * 4 : (o % 8) * 4 + 4, :]
            tt[o, 8 * v + 4 : 8 * v + 8, :] = jnp.zeros((4, TD), F32)

    pl.semaphore_wait(barrier, MIC + DP // 2 + 1)

    def wave_copy(b, j, slot, dev):
        return remote(wblk.at[b], gath.at[slot, b], g_send.at[MIC * b + j], g_recv.at[MIC * b + slot], d, dev)

    def head_copy(j, slot, dev):
        return remote(heads.at[mu], heads.at[slot], h_send.at[j], h_recv.at[slot], d, dev)

    def head_first():
        return remote(head, heads.at[mu], h_send.at[0], h_recv.at[mu], prev, mu)

    head_first().start()
    for j in range(1, MIC):
        wave_copy(0, j, mu, other_m(j)).start()
    gath[mu] = wblk[...]
    head_first().wait_recv()
    for j in range(1, MIC):
        head_copy(j, mu, other_m(j)).start()
    for j in range(1, MIC):
        wave_copy(1, j, mu, other_m(j)).start()

    last = d == DP - 1
    tap128 = iota((128, 128), 1) == iota((128, 128), 0) % 16
    end = iota((128, TD), 1) == TD - 1

    def encode(b):
        for q in range(4):
            x = jnp.concatenate([gath[2 * q, b], gath[2 * q + 1, b]], axis=0).astype(F32)
            near = jnp.concatenate(
                [
                    jnp.broadcast_to(heads[2 * q + p, 4 * b + m : 4 * b + m + 1, :], (16, 128))
                    for p in range(2)
                    for m in range(4)
                ],
                axis=0,
            )
            near = jnp.where(last, 0.0, near)
            column = jnp.sum(jnp.where(tap128, near, 0.0), axis=1, keepdims=True)
            moved = jnp.where(end, column, pltpu.roll(x, TD - 1, axis=1))
            frames[b, q, 0:128, :] = x.astype(BF16)
            frames[b, q, 128:256, :] = moved.astype(BF16)
        for half in range(2):
            a0 = jnp.dot(fb[...], frames[b, 2 * half], preferred_element_type=F32)
            a1 = jnp.dot(fb[...], frames[b, 2 * half + 1], preferred_element_type=F32)
            z = jnp.concatenate(
                [a0.reshape(8, 4, 2, 8, TD), a1.reshape(8, 4, 2, 8, TD)], axis=3
            ).astype(BF16)
            for v in range(2):
                zz[8 * b : 8 * b + 8, v, :, 16 * half : 16 * half + 16, :] = z[:, :, v]

    lane32 = iota((32, 128), 1)
    upper = iota((32, 128), 0) <= lane32 % 32
    row8 = iota((8, 128), 0)
    own8 = row8 == iota((8, 128), 1) // 32

    def group_sums(o):
        t_hi, t_lo = split(tt[o])
        lhs[512:768, :] = zz[o].reshape(256, TD)
        lhs[768:800, :] = jnp.concatenate([t_hi, t_lo], axis=0).astype(BF16)
        for g in range(4):
            for k, ref in enumerate((ms, mn)):
                mask = jnp.broadcast_to(ref[pl.ds(4 * o + g, 1), :], (32, TD)).astype(BF16)
                for v in range(2):
                    part = zz[o, v, g] * mask
                    at = 128 * v + 32 * g
                    lhs[256 * k + at : 256 * k + at + 32, :] = part
                    yy[o, k, at : at + 32, :] = part
        out = nt_dot(lhs[...], zz[o].reshape(256, TD))
        for kind in range(3):
            value = jnp.zeros((32, 128), F32)
            for g in range(4):
                re = out[256 * kind + 32 * g : 256 * kind + 32 * g + 32]
                im = out[256 * kind + 128 + 32 * g : 256 * kind + 160 + 32 * g]
                one = jnp.where(upper, re[:, :128] + im[:, 128:], im[:, :128] - re[:, 128:])
                value = jnp.where(lane32 // 32 == g, one, value)
            sb[o, 32 * kind : 32 * kind + 32, :] = value
        t0 = out[768:776] + out[784:792]
        t1 = out[776:784] + out[792:800]
        d_r = jnp.sum(jnp.where(own8, t0[:, :128] + t1[:, 128:], 0.0), axis=0, keepdims=True)
        d_i = jnp.sum(jnp.where(own8, t0[:, 128:] - t1[:, :128], 0.0), axis=0, keepdims=True)
        sb[o, 96:104, :] = jnp.where(row8 == 0, d_r, jnp.where(row8 == 1, d_i, 0.0))

    def sum_copy(o, slot, sem, dev):
        return remote(sb.at[o], rb.at[slot], s_send.at[sem], s_recv.at[slot], dev, mu)

    def add_slot(o, slot):
        sum_copy(o, slot, slot, core).wait_recv()
        sb[o] = sb[o] + rb[slot]

    for b in range(2):
        for j in range(1, MIC):
            wave_copy(b, j, other_m(j), mu).wait_recv()
        if b == 0:
            for j in range(1, MIC):
                head_copy(j, other_m(j), mu).wait_recv()
        encode(b)
        here = jnp.where(at_z // 2 == b, 1, 0)

        @pl.loop(0, 8)
        def _(i):
            mine = table(i, [0, 0, 1, 0, 1, 0, 1, 1])
            k = table(i, [0, 1, 0, 2, 1, 3, 2, 3])
            to = 2 * (2 * b + (at_z + k // 2 + here) % 2) + (at_x + 1 + k) % 2
            o = 2 * to + (at_c + 1 + mine) % 2
            group_sums(o)

            @pl.when(mine == 0)
            def _():
                sum_copy(o, to, to, core).start()

            @pl.when(mine == 1)
            def _():
                add_slot(o, to)

            @pl.when((mine == 1) & (to != chip))
            def _():
                sum_copy(o, 8 + chip, 8 + to, o).start()

    for k in range(7):
        add_slot(d, 8 + others[k] // 2)
    pick = jnp.where(d < DP // 2, pick_ref[0], pick_ref[1])
    speech, noise, w_r, w_i = solve(sb[d], pick)
    pay[d, 0:32, :] = speech
    pay[d, 32:64, :] = noise
    pay[d, 64:72, :] = jnp.where(row8 == 0, w_r, jnp.where(row8 == 1, w_i, 0.0))

    def pay_copy(o, sem, dev):
        return remote(pay.at[o], pay.at[o], p_send.at[sem], p_recv.at[o], dev, mu)

    for k, dev in enumerate([core] + others):
        pay_copy(d, k, dev).start()

    def group_grads(o):
        b = o // 8
        f0 = (o % 8) * 4
        w_r = jnp.where(own8, pay[o, 64:65, :], 0.0)
        w_i = jnp.where(own8, pay[o, 65:66, :], 0.0)
        wr_hi, wr_lo = split(w_r)
        wi_hi, wi_lo = split(w_i)

        def wide(p, q):
            return jnp.concatenate([p, q], axis=1)

        first = jnp.concatenate([wide(wr_hi, wi_hi), wide(-wi_hi, wr_hi)], axis=0)
        second = jnp.concatenate([wide(wr_lo, wi_lo), wide(-wi_lo, wr_lo)], axis=0)
        left = jnp.concatenate([first, second], axis=0)
        both = jnp.dot(left.astype(BF16), zz[o].reshape(256, TD), preferred_element_type=F32)
        enh = both[0:16] + both[16:32]
        for g in range(4):
            enh_ref[b, 0, pl.ds(f0 + g, 1), :] = enh[g : g + 1, :]
            enh_ref[b, 1, pl.ds(f0 + g, 1), :] = enh[8 + g : 9 + g, :]
        e_hi, e_lo = split(GRAD_SCALE * (enh - tt[o]))
        s_r, s_i = unpack_blocks(pay[o, 0:32, :])
        n_r, n_i = unpack_blocks(pay[o, 32:64, :])
        parts = []
        for r, i in ((s_r, s_i), (n_r, n_i)):
            r_hi, r_lo = split(r)
            i_hi, i_lo = split(i)
            for p, q in ((r_hi, i_hi), (r_lo, i_lo)):
                parts.append(jnp.concatenate([wide(p, -q), wide(q, p)], axis=0).astype(BF16))
        e_rows = jnp.concatenate([e_hi, e_hi, e_lo], axis=0).astype(BF16)
        w_cols = jnp.concatenate([first, second, first], axis=0).T.astype(BF16)
        sg = jnp.dot(w_cols, e_rows, preferred_element_type=F32)
        for k in range(2):
            for part in parts[2 * k : 2 * k + 2]:
                sg = sg + jnp.dot(part, yy[o, k], preferred_element_type=F32)
        for g in range(4):
            place = pl.ds(pl.multiple_of(16 * (f0 + g), 16), 16)
            for q in range(4):
                at = 32 * g + 8 * q
                sgq[b, q, place, :] = jnp.concatenate(
                    [sg[at : at + 8], sg[128 + at : 136 + at]], axis=0
                ).astype(BF16)

    spread = [(0, 0, 0), (0, 0, 1), (0, 1, 0), (1, 0, 0), (3, 0, 0), (0, 1, 1), (1, 1, 0), (3, 1, 0),
              (1, 0, 1), (3, 0, 1), (2, 0, 0), (2, 1, 0), (1, 1, 1), (3, 1, 1), (2, 0, 1), (2, 1, 1)]

    @pl.loop(0, DP)
    def _(i):
        dz = table(i, [k[0] for k in spread])
        dx = table(i, [k[1] for k in spread])
        dc = table(i, [k[2] for k in spread])
        o = rel(dz, dx, dc)

        @pl.when(i > 0)
        def _():
            pay_copy(o, 0, core).wait_recv()

        @pl.when((i > 0) & (dc == 0))
        def _():
            pay_copy(o, 8 + o // 2, core).start()

        group_grads(o)

    acc = jnp.zeros((512, 256), F32)
    for b in range(2):
        for q in range(4):
            acc = acc + nt_dot(sgq[b, q], frames[b, q])
    keep = iota((512, 256), 0) % 8 == (iota((512, 256), 1) % 128) // 16
    rows = jnp.sum(jnp.where(keep, acc, 0.0).reshape(64, 8, 256), axis=1)
    at, lane = iota((256, 128), 0), iota((256, 128), 1)
    tap = (at // 128) * 16 + at % 16
    part = jnp.zeros((16, 128), F32)
    for p in range(4):
        place = jnp.where((lane // 32 == p) & (lane % 32 == tap), 1.0, 0.0)
        part = part + dot_f32(rows[16 * p : 16 * p + 16], place)
    fg[d] = part

    def grad_copy(j, slot, dev):
        return remote(fg.at[d], fg.at[slot], f_send.at[j], f_recv.at[slot], dev, mu)

    for j in range(1, DP):
        grad_copy(j, d, other_d(j)).start()
    for j in range(1, DP):
        grad_copy(j, other_d(j), d).wait_recv()
    result = fg[0]
    for j in range(1, DP):
        result = result + fg[j]
    turned = result.T
    grad_ref[...] = jnp.concatenate([turned[32 * p : 32 * p + 32] for p in range(4)], axis=1)

    head_first().wait_send()
    for j in range(1, MIC):
        wave_copy(0, j, mu, mu).wait_send()
        wave_copy(1, j, mu, mu).wait_send()
        head_copy(j, mu, mu).wait_send()
    for k in range(8):
        sum_copy(d, 0, k, core).wait_send()
        pay_copy(d, k, core).wait_send()
    for k in range(7):
        sum_copy(d, 0, 8 + others[k] // 2, core).wait_send()
        pay_copy(d, 8 + others[k] // 2, core).wait_send()
    for j in range(1, DP):
        grad_copy(j, d, d).wait_send()


def local(waveform, filters, speech_mask, noise_mask, target, ref_mic):
    vmem = pl.BlockSpec(memory_space=pltpu.VMEM)
    dma = pltpu.SemaphoreType.DMA
    enhanced, grad = pl.pallas_call(
        body,
        out_shape=(
            jax.ShapeDtypeStruct((2, 2, 32, TD), F32),
            jax.ShapeDtypeStruct((32, 64), F32),
        ),
        in_specs=[vmem] * 5 + [pl.BlockSpec(memory_space=pltpu.SMEM)],
        out_specs=(vmem, vmem),
        scratch_shapes=[
            pltpu.VMEM((2, 64, TD), BF16),
            pltpu.VMEM((8, 128), F32),
            pltpu.VMEM((MIC, 2, 64, TD), BF16),
            pltpu.VMEM((MIC, 8, 128), F32),
            pltpu.VMEM((2, 4, 256, TD), BF16),
            pltpu.VMEM((DP, 2, 4, 32, TD), BF16),
            pltpu.VMEM((DP, 2, 256, TD), BF16),
            pltpu.VMEM((800, TD), BF16),
            pltpu.VMEM((DP, ROWS, 128), F32),
            pltpu.VMEM((DP, ROWS, 128), F32),
            pltpu.VMEM((DP, PAY, 128), F32),
            pltpu.VMEM((2, 4, 512, TD), BF16),
            pltpu.VMEM((DP, 16, 128), F32),
            pltpu.VMEM((DP, 16, TD), F32),
            pltpu.VMEM((64, TD), F32),
            pltpu.VMEM((64, TD), F32),
            pltpu.VMEM((512, 256), BF16),
            dma((2 * MIC,)), dma((2 * MIC,)), dma((MIC,)), dma((MIC,)),
            dma((DP,)), dma((DP,)), dma((DP,)), dma((DP,)), dma((DP,)), dma((DP,)),
        ],
        compiler_params=pltpu.CompilerParams(
            collective_id=0, has_side_effects=True, vmem_limit_bytes=60 * 1024 * 1024
        ),
    )(waveform, filters.T, speech_mask, noise_mask, target, ref_mic)
    return (enhanced, grad.T)


def solution(mesh):
    in_specs = (
        P(None, "mic", "dp"),
        P("mic", None),
        P(None, "mic", "dp"),
        P(None, "mic", "dp"),
        P(None, None, "mic", "dp"),
        P(),
    )
    out_specs = (P(None, None, "mic", "dp"), P("mic", None))
    return jax.shard_map(local, mesh=mesh, in_specs=in_specs, out_specs=out_specs, check_vma=False)
```

time: 68.7 us -> 55.4 us (0.81)
  Pallas kernels: 61.4 us -> 52.5 us
  local copies, waits for them, and re-layouts: 5.68 us -> 2.18 us
    pallas_call x1, Pallas kernels: 61.4 us -> 52.5 us  [local(): pl.pallas_call(body, out_shape=(jax.ShapeDtypeStruct((2, 2, 32, TD), F32)...]
    reshape x3 -> x0, local copies, waits for them, and re-layouts: 2.05 us -> none  [the longest x1 1.23 us: local(): waveform.reshape(2, 4, TD, 16).transpose(0, 1, 3, 2).reshape(2, 64, TD)]
    transpose x1 -> x0, local copies, waits for them, and re-layouts: 0.82 us -> none  [local(): waveform.reshape(2, 4, TD, 16).transpose(0, 1, 3, 2).reshape(2, 64, TD)]
    unnamed x7 -> x4, local copies, waits for them, and re-layouts: 2.04 us -> 2.18 us
where the time goes in v3:
time: 55.4 us; the launch traced here: 55.3 us
  Pallas kernels  52.5 us (95%)
  local copies, waits for them, and re-layouts  2.18 us (4%)
  between operations  0.65 us (1%)
    pallas_call x1, Pallas kernels, local(): pl.pallas_call(body, out_shape=(jax.ShapeDtypeStruct((2, 2, 32, TD), F32)...  52.5 us
    unnamed x4, local copies, waits for them, and re-layouts  2.18 us

profile of v3, /device:TPU:1, one launch (start us, length us, event | category | flops | bytes accessed | tf_op | source)
XLA Modules:
  0.0 55.3 jit_solution(1229678978633876252)
XLA Ops:
  0.6 52.5 %shard_map.77 = (f32[2,2,32,256]{3,2,1,0:T(8,128)}, f32[32,64]{1,0:T(8,128)}) custom-call(bf16[2,4,4096]{2,1,0:T(4,128)(2,1)} %wave_ref.1, bf16[32,64]{1,0:T(8,128)(2,1)} %bitcast.3, bf16[2,32,256]{2,1,0:T(8,128)(2,1)} %smask_ref.1, bf16[2,32,256]{2,1,0:T(8,128)(2,1)} %nmask_ref.1, f32[2,2,32,256]{3,2,1,0:T(8,128)} %target_ref.1, s32[2]{0:T(128)} %pick_ref.1), custom_call_target="tpu_custom_call" | custom-call | tf_op jit(solution)/shard_map/pallas_call | solution.py:489
  53.1 0.0 copy-start
  53.1 1.6 %copy.10 = f32[2,2,32,256]{3,2,1,0:T(8,128)} copy(f32[2,2,32,256]{3,2,1,0:T(8,128)} %get-tuple-element.8) | data formatting | bytes 262144
  54.7 0.0 copy-done
  54.7 0.6 %copy.11 = f32[64,32]{0,1:T(8,128)} copy(f32[64,32]{0,1:T(8,128)S(1)} %bitcast.2) | data formatting | bytes 16384
Async XLA Ops:
  53.1 1.6 %copy-start = (f32[32,64]{1,0:T(8,128)S(1)}, f32[32,64]{1,0:T(8,128)}, u32[]{:S(2)}) copy-start(f32[32,64]{1,0:T(8,128)} %get-tuple-element.5) | copy-start | bytes 24580

commit v4 on v3

--- a/solution.py
+++ b/solution.py
@@ -47,6 +47,14 @@
     real = jnp.where(rows <= lanes, blocks, turned)
     imag = jnp.where(rows > lanes, blocks, jnp.where(rows < lanes, -turned, 0.0))
     return real, imag
+
+
+def unpack_four(packed):
+    row, col = iota((32, 128), 0), iota((32, 128), 1) % 32
+    turned = fold4(diagonal_blocks(packed).T)
+    real = jnp.where(row <= col, packed, turned)
+    negated = jnp.where(row > col, -packed, jnp.where(row < col, turned, 0.0))
+    return real, negated
 
 
 def complex_right(real, imag):
@@ -286,11 +294,13 @@
             near = jnp.where(last, 0.0, near)
             column = jnp.sum(jnp.where(tap128, near, 0.0), axis=1, keepdims=True)
             moved = jnp.where(end, column, pltpu.roll(x, TD - 1, axis=1))
-            frames[b, q, 0:128, :] = x.astype(BF16)
-            frames[b, q, 128:256, :] = moved.astype(BF16)
+            piece = slice(TD * (4 * b + q), TD * (4 * b + q) + TD)
+            frames[0:128, piece] = x.astype(BF16)
+            frames[128:256, piece] = moved.astype(BF16)
         for half in range(2):
-            a0 = jnp.dot(fb[...], frames[b, 2 * half], preferred_element_type=F32)
-            a1 = jnp.dot(fb[...], frames[b, 2 * half + 1], preferred_element_type=F32)
+            at = TD * (4 * b + 2 * half)
+            a0 = jnp.dot(fb[...], frames[:, at : at + TD], preferred_element_type=F32)
+            a1 = jnp.dot(fb[...], frames[:, at + TD : at + 2 * TD], preferred_element_type=F32)
             z = jnp.concatenate(
                 [a0.reshape(8, 4, 2, 8, TD), a1.reshape(8, 4, 2, 8, TD)], axis=3
             ).astype(BF16)
@@ -302,19 +312,20 @@
     row8 = iota((8, 128), 0)
     own8 = row8 == iota((8, 128), 1) // 32
 
-    def group_sums(o):
+    def group_sums(o, w):
         t_hi, t_lo = split(tt[o])
-        lhs[512:768, :] = zz[o].reshape(256, TD)
-        lhs[768:800, :] = jnp.concatenate([t_hi, t_lo], axis=0).astype(BF16)
+        lhs[w, 512:768, :] = zz[o].reshape(256, TD)
+        lhs[w, 768:800, :] = jnp.concatenate([t_hi, t_lo], axis=0).astype(BF16)
         for g in range(4):
             for k, ref in enumerate((ms, mn)):
                 mask = jnp.broadcast_to(ref[pl.ds(4 * o + g, 1), :], (32, TD)).astype(BF16)
                 for v in range(2):
                     part = zz[o, v, g] * mask
                     at = 128 * v + 32 * g
-                    lhs[256 * k + at : 256 * k + at + 32, :] = part
-                    yy[o, k, at : at + 32, :] = part
-        out = nt_dot(lhs[...], zz[o].reshape(256, TD))
+                    lhs[w, 256 * k + at : 256 * k + at + 32, :] = part
+                    row = 64 * k + 32 * ((v + g) % 2)
+                    yy[o, g, row : row + 32, :] = part
+        out = nt_dot(lhs[w], zz[o].reshape(256, TD))
         for kind in range(3):
             value = jnp.zeros((32, 128), F32)
             for g in range(4):
@@ -345,32 +356,50 @@
         encode(b)
         here = jnp.where(at_z // 2 == b, 1, 0)
 
-        @pl.loop(0, 8)
+        def target(k, mine):
+            to = 2 * (2 * b + (at_z + k // 2 + here) % 2) + (at_x + 1 + k) % 2
+            return to, 2 * to + (at_c + 1 + mine) % 2
+
+        def give(to, o):
+            sum_copy(o, to, to, core).start()
+
+        def keep(to, o):
+            add_slot(o, to)
+
+            @pl.when(to != chip)
+            def _():
+                sum_copy(o, 8 + chip, 8 + to, o).start()
+
+        @pl.loop(0, 4)
         def _(i):
-            mine = table(i, [0, 0, 1, 0, 1, 0, 1, 1])
-            k = table(i, [0, 1, 0, 2, 1, 3, 2, 3])
-            to = 2 * (2 * b + (at_z + k // 2 + here) % 2) + (at_x + 1 + k) % 2
-            o = 2 * to + (at_c + 1 + mine) % 2
-            group_sums(o)
-
-            @pl.when(mine == 0)
-            def _():
-                sum_copy(o, to, to, core).start()
-
-            @pl.when(mine == 1)
-            def _():
-                add_slot(o, to)
-
-            @pl.when((mine == 1) & (to != chip))
-            def _():
-                sum_copy(o, 8 + chip, 8 + to, o).start()
+            to_a, o_a = target(table(i, [0, 2, 3, 2]), table(i, [0, 0, 0, 1]))
+            to_b, o_b = target(table(i, [1, 0, 1, 3]), table(i, [0, 1, 1, 1]))
+            group_sums(o_a, 0)
+            group_sums(o_b, 1)
+
+            @pl.when(i < 3)
+            def _():
+                give(to_a, o_a)
+
+            @pl.when(i == 3)
+            def _():
+                keep(to_a, o_a)
+
+            @pl.when(i == 0)
+            def _():
+                give(to_b, o_b)
+
+            @pl.when(i > 0)
+            def _():
+                keep(to_b, o_b)
 
     for k in range(7):
         add_slot(d, 8 + others[k] // 2)
     pick = jnp.where(d < DP // 2, pick_ref[0], pick_ref[1])
     speech, noise, w_r, w_i = solve(sb[d], pick)
-    pay[d, 0:32, :] = speech
-    pay[d, 32:64, :] = noise
+    left_half = lane32 < 64
+    pay[d, 0:32, :] = jnp.where(left_half, speech, pltpu.roll(noise, 64, axis=1))
+    pay[d, 32:64, :] = jnp.where(left_half, pltpu.roll(speech, 64, axis=1), noise)
     pay[d, 64:72, :] = jnp.where(row8 == 0, w_r, jnp.where(row8 == 1, w_i, 0.0))
 
     def pay_copy(o, sem, dev):
@@ -399,60 +428,70 @@
             enh_ref[b, 0, pl.ds(f0 + g, 1), :] = enh[g : g + 1, :]
             enh_ref[b, 1, pl.ds(f0 + g, 1), :] = enh[8 + g : 9 + g, :]
         e_hi, e_lo = split(GRAD_SCALE * (enh - tt[o]))
-        s_r, s_i = unpack_blocks(pay[o, 0:32, :])
-        n_r, n_i = unpack_blocks(pay[o, 32:64, :])
-        parts = []
-        for r, i in ((s_r, s_i), (n_r, n_i)):
-            r_hi, r_lo = split(r)
-            i_hi, i_lo = split(i)
-            for p, q in ((r_hi, i_hi), (r_lo, i_lo)):
-                parts.append(jnp.concatenate([wide(p, -q), wide(q, p)], axis=0).astype(BF16))
         e_rows = jnp.concatenate([e_hi, e_hi, e_lo], axis=0).astype(BF16)
-        w_cols = jnp.concatenate([first, second, first], axis=0).T.astype(BF16)
-        sg = jnp.dot(w_cols, e_rows, preferred_element_type=F32)
-        for k in range(2):
-            for part in parts[2 * k : 2 * k + 2]:
-                sg = sg + jnp.dot(part, yy[o, k], preferred_element_type=F32)
+        w_cols = jnp.concatenate([first, second, first], axis=0).T
+        even = (lane32 // 32) % 2 == 0
         for g in range(4):
+            if g % 2 == 0:
+                re, neg = unpack_four(pay[o, 16 * g : 16 * g + 32, :])
+            shift = 32 if g % 2 == 0 else 96
+            own = even if g % 2 == 0 else ~even
+            top = jnp.where(own, re, pltpu.roll(neg, shift, axis=1))
+            bottom = jnp.where(own, -neg, pltpu.roll(re, shift, axis=1))
+            hi, lo = split(jnp.concatenate([top, bottom], axis=0))
+            cols = jnp.concatenate(
+                [w_cols[32 * g : 32 * g + 32], w_cols[128 + 32 * g : 160 + 32 * g]], axis=0
+            )
+            lhs_g = jnp.concatenate([wide(hi, cols), wide(lo, jnp.zeros_like(cols))], axis=0)
+            rhs_g = jnp.concatenate([yy[o, g], e_rows], axis=0)
+            both = jnp.dot(lhs_g.astype(BF16), rhs_g, preferred_element_type=F32)
+            sg = both[0:64] + both[64:128]
             place = pl.ds(pl.multiple_of(16 * (f0 + g), 16), 16)
             for q in range(4):
-                at = 32 * g + 8 * q
-                sgq[b, q, place, :] = jnp.concatenate(
-                    [sg[at : at + 8], sg[128 + at : 136 + at]], axis=0
+                sgq[place, pl.ds(pl.multiple_of(TD * (4 * b + q), TD), TD)] = jnp.concatenate(
+                    [sg[8 * q : 8 * q + 8], sg[32 + 8 * q : 40 + 8 * q]], axis=0
                 ).astype(BF16)
 
-    spread = [(0, 0, 0), (0, 0, 1), (0, 1, 0), (1, 0, 0), (3, 0, 0), (0, 1, 1), (1, 1, 0), (3, 1, 0),
-              (1, 0, 1), (3, 0, 1), (2, 0, 0), (2, 1, 0), (1, 1, 1), (3, 1, 1), (2, 0, 1), (2, 1, 1)]
-
-    @pl.loop(0, DP)
+    spread = [
+        [(0, 0, 0), (0, 1, 0), (3, 0, 0), (1, 1, 0), (1, 0, 1), (2, 0, 0), (1, 1, 1), (2, 0, 1)],
+        [(0, 0, 1), (1, 0, 0), (0, 1, 1), (3, 1, 0), (3, 0, 1), (2, 1, 0), (3, 1, 1), (2, 1, 1)],
+    ]
+
+    @pl.loop(0, DP // 2)
     def _(i):
-        dz = table(i, [k[0] for k in spread])
-        dx = table(i, [k[1] for k in spread])
-        dc = table(i, [k[2] for k in spread])
-        o = rel(dz, dx, dc)
-
-        @pl.when(i > 0)
-        def _():
-            pay_copy(o, 0, core).wait_recv()
-
-        @pl.when((i > 0) & (dc == 0))
-        def _():
-            pay_copy(o, 8 + o // 2, core).start()
-
-        group_grads(o)
-
-    acc = jnp.zeros((512, 256), F32)
-    for b in range(2):
-        for q in range(4):
-            acc = acc + nt_dot(sgq[b, q], frames[b, q])
+        pair = []
+        for column in spread:
+            dz = table(i, [k[0] for k in column])
+            dx = table(i, [k[1] for k in column])
+            dc = table(i, [k[2] for k in column])
+            pair.append((rel(dz, dx, dc), dc))
+        for o, dc in pair:
+
+            @pl.when(o != d)
+            def _():
+                pay_copy(o, 0, core).wait_recv()
+
+            @pl.when((o != d) & (dc == 0))
+            def _():
+                pay_copy(o, 8 + o // 2, core).start()
+
+        for o, dc in pair:
+            group_grads(o)
+
+    acc = nt_dot(sgq[...], frames[...])
     keep = iota((512, 256), 0) % 8 == (iota((512, 256), 1) % 128) // 16
     rows = jnp.sum(jnp.where(keep, acc, 0.0).reshape(64, 8, 256), axis=1)
-    at, lane = iota((256, 128), 0), iota((256, 128), 1)
-    tap = (at // 128) * 16 + at % 16
+    lane16 = iota((16, 128), 1)
+    halves = []
+    for half in (rows[:, :128], rows[:, 128:]):
+        for step in (64, 32, 16):
+            half = half + pltpu.roll(half, step, axis=1)
+        halves.append(half)
     part = jnp.zeros((16, 128), F32)
     for p in range(4):
-        place = jnp.where((lane // 32 == p) & (lane % 32 == tap), 1.0, 0.0)
-        part = part + dot_f32(rows[16 * p : 16 * p + 16], place)
+        at = slice(16 * p, 16 * p + 16)
+        one = jnp.where((lane16 // 16) % 2 == 0, halves[0][at], halves[1][at])
+        part = jnp.where(lane16 // 32 == p, one, part)
     fg[d] = part
 
     def grad_copy(j, slot, dev):
@@ -499,14 +538,14 @@
             pltpu.VMEM((8, 128), F32),
             pltpu.VMEM((MIC, 2, 64, TD), BF16),
             pltpu.VMEM((MIC, 8, 128), F32),
-            pltpu.VMEM((2, 4, 256, TD), BF16),
+            pltpu.VMEM((256, 8 * TD), BF16),
             pltpu.VMEM((DP, 2, 4, 32, TD), BF16),
-            pltpu.VMEM((DP, 2, 256, TD), BF16),
-            pltpu.VMEM((800, TD), BF16),
+            pltpu.VMEM((DP, 4, 128, TD), BF16),
+            pltpu.VMEM((2, 800, TD), BF16),
             pltpu.VMEM((DP, ROWS, 128), F32),
             pltpu.VMEM((DP, ROWS, 128), F32),
             pltpu.VMEM((DP, PAY, 128), F32),
-            pltpu.VMEM((2, 4, 512, TD), BF16),
+            pltpu.VMEM((512, 8 * TD), BF16),
             pltpu.VMEM((DP, 16, 128), F32),
             pltpu.VMEM((DP, 16, TD), F32),
             pltpu.VMEM((64, TD), F32),

time: 55.4 us -> 52.5 us (0.948)
  Pallas kernels: 52.5 us -> 49.6 us
    pallas_call x1, Pallas kernels: 52.5 us -> 49.6 us  [local(): pl.pallas_call(body, out_shape=(jax.ShapeDtypeStruct((2, 2, 32, TD), F32)...]
where the time goes in v4:
time: 52.5 us; the launch traced here: 52.4 us
  Pallas kernels  49.6 us (94%)
  local copies, waits for them, and re-layouts  2.18 us (4%)
  between operations  0.65 us (1%)
    pallas_call x1, Pallas kernels, local(): pl.pallas_call(body, out_shape=(jax.ShapeDtypeStruct((2, 2, 32, TD), F32)...  49.6 us
    unnamed x4, local copies, waits for them, and re-layouts  2.18 us

profile of v4, /device:TPU:1, one launch (start us, length us, event | category | flops | bytes accessed | tf_op | source)
XLA Modules:
  0.0 52.4 jit_solution(17334325806527832895)
XLA Ops:
  0.6 49.6 %shard_map.77 = (f32[2,2,32,256]{3,2,1,0:T(8,128)}, f32[32,64]{1,0:T(8,128)}) custom-call(bf16[2,4,4096]{2,1,0:T(4,128)(2,1)} %wave_ref.1, bf16[32,64]{1,0:T(8,128)(2,1)} %bitcast.3, bf16[2,32,256]{2,1,0:T(8,128)(2,1)} %smask_ref.1, bf16[2,32,256]{2,1,0:T(8,128)(2,1)} %nmask_ref.1, f32[2,2,32,256]{3,2,1,0:T(8,128)} %target_ref.1, s32[2]{0:T(128)} %pick_ref.1), custom_call_target="tpu_custom_call" | custom-call | tf_op jit(solution)/shard_map/pallas_call | solution.py:528
  50.2 0.0 copy-start
  50.2 1.6 %copy.10 = f32[2,2,32,256]{3,2,1,0:T(8,128)} copy(f32[2,2,32,256]{3,2,1,0:T(8,128)} %get-tuple-element.8) | data formatting | bytes 262144
  51.8 0.0 copy-done
  51.8 0.6 %copy.11 = f32[64,32]{0,1:T(8,128)} copy(f32[64,32]{0,1:T(8,128)S(1)} %bitcast.2) | data formatting | bytes 16384
Async XLA Ops:
  50.2 1.6 %copy-start = (f32[32,64]{1,0:T(8,128)S(1)}, f32[32,64]{1,0:T(8,128)}, u32[]{:S(2)}) copy-start(f32[32,64]{1,0:T(8,128)} %get-tuple-element.5) | copy-start | bytes 24580

commit v5 on v4

--- a/solution.py
+++ b/solution.py
@@ -14,17 +14,12 @@
 GRAD_SCALE = 2.0 * 64.0 / (2 * 256 * FRAME_TOTAL)
 F32 = jnp.float32
 BF16 = jnp.bfloat16
-HIGHEST = lax.Precision.HIGHEST
 ROWS = 104
 PAY = 72
 
 
 def iota(shape, axis):
     return lax.broadcasted_iota(jnp.int32, shape, axis)
-
-
-def dot_f32(a, b):
-    return jnp.dot(a, b, precision=HIGHEST, preferred_element_type=F32)
 
 
 def tile4(x):
@@ -38,15 +33,6 @@
 
 def fold4(x):
     return (x[0:32] + x[32:64]) + (x[64:96] + x[96:128])
-
-
-def unpack_blocks(packed):
-    rows, lanes = iota((128, 128), 0) % 32, iota((128, 128), 1) % 32
-    blocks = diagonal_blocks(packed)
-    turned = blocks.T
-    real = jnp.where(rows <= lanes, blocks, turned)
-    imag = jnp.where(rows > lanes, blocks, jnp.where(rows < lanes, -turned, 0.0))
-    return real, imag
 
 
 def unpack_four(packed):
@@ -55,12 +41,6 @@
     real = jnp.where(row <= col, packed, turned)
     negated = jnp.where(row > col, -packed, jnp.where(row < col, turned, 0.0))
     return real, negated
-
-
-def complex_right(real, imag):
-    return jnp.concatenate(
-        [jnp.concatenate([real, imag], axis=1), jnp.concatenate([-imag, real], axis=1)], axis=0
-    )
 
 
 def inverse(a_r, a_i):
@@ -85,29 +65,67 @@
     return a_r, a_i
 
 
+def thirds(x):
+    one = x.astype(BF16).astype(F32)
+    two = (x - one).astype(BF16).astype(F32)
+    return one, two, x - one - two
+
+
+def complex_blocks(real, imag):
+    keep = iota((128, 128), 0) // 32 == iota((128, 128), 1) // 32
+    r = jnp.where(keep, tile4(real), 0.0).astype(BF16)
+    i = jnp.where(keep, tile4(imag), 0.0).astype(BF16)
+    return jnp.concatenate(
+        [jnp.concatenate([r, i], axis=1), jnp.concatenate([-i, r], axis=1)], axis=0
+    )
+
+
+def times(a_r, a_i, b_r, b_i):
+    a = thirds(jnp.concatenate([a_r, a_i], axis=1))
+    reals, imags = thirds(b_r), thirds(b_i)
+    out = None
+    for k in range(2, -1, -1):
+        rows = jnp.concatenate(a[: 3 - k], axis=0).astype(BF16)
+        part = jnp.dot(rows, complex_blocks(reals[k], imags[k]), preferred_element_type=F32)
+        for m in range(2 - k, -1, -1):
+            one = part[32 * m : 32 * m + 32]
+            out = one if out is None else out + one
+    return out[:, :128], out[:, 128:]
+
+
+def group_totals(x):
+    ones = jnp.where(iota((128, 128), 0) // 32 == iota((128, 128), 1) // 32, 1.0, 0.0).astype(BF16)
+    n = x.shape[0]
+    rows = jnp.concatenate(thirds(x), axis=0).astype(BF16)
+    out = jnp.dot(rows, ones, preferred_element_type=F32)
+    return out[0:n] + (out[n : 2 * n] + out[2 * n :])
+
+
 def solve(total, pick):
     lane = iota((32, 128), 1)
     row = iota((32, 128), 0)
-    eye = jnp.where(row == lane % 32, 1.0, 0.0)
+    eye = row == lane % 32
     inv_t = 1.0 / FRAME_TOTAL
-    s_r, s_i = [fold4(x) for x in unpack_blocks(total[0:32])]
-    n_r, n_i = [fold4(x) for x in unpack_blocks(total[32:64])]
-    cb_r, cb_i = unpack_blocks(total[64:96])
+
+    def column_sum(x):
+        return jnp.sum(x, axis=0, keepdims=True)
+
+    s_r, s_neg = unpack_four(total[0:32])
+    n_r, n_neg = unpack_four(total[32:64])
+    k_r, k_neg = unpack_four(total[64:96])
     d_r, d_i = total[96:97], total[97:98]
-    s_r = s_r * inv_t + LOAD * eye
-    s_i = s_i * inv_t
-    m_r, m_i = inverse(n_r * inv_t + LOAD * eye, n_i * inv_t)
-    right_m = complex_right(diagonal_blocks(m_r), diagonal_blocks(m_i))
-    xh = dot_f32(jnp.concatenate([s_r, s_i], axis=1), right_m)
-    xh_r, xh_i = xh[:, :128], xh[:, 128:]
+    s_r = s_r * inv_t + jnp.where(eye, LOAD, 0.0)
+    s_i = s_neg * -inv_t
+    m_r, m_i = inverse(n_r * inv_t + jnp.where(eye, LOAD, 0.0), n_neg * -inv_t)
+    xh_r, xh_i = times(s_r, s_i, m_r, m_i)
+    q_r, q_i = times(m_r, m_i, xh_r, xh_i)
     at_ref = row == pick
-    conj_c_r = jnp.sum(jnp.where(at_ref, xh_r, 0.0), axis=0, keepdims=True)
-    conj_c_i = jnp.sum(jnp.where(at_ref, xh_i, 0.0), axis=0, keepdims=True)
-    sref_r = jnp.sum(jnp.where(at_ref, s_r, 0.0), axis=0, keepdims=True)
-    sref_i = jnp.sum(jnp.where(at_ref, s_i, 0.0), axis=0, keepdims=True)
-    ones = jnp.where(iota((128, 128), 0) // 32 == iota((128, 128), 1) // 32, 1.0, 0.0)
-    diag = jnp.sum(xh_r * eye, axis=0, keepdims=True)
-    first = dot_f32(
+    conj_c_r = column_sum(jnp.where(at_ref, xh_r, 0.0))
+    conj_c_i = column_sum(jnp.where(at_ref, xh_i, 0.0))
+    sref_r = column_sum(jnp.where(at_ref, s_r, 0.0))
+    sref_i = column_sum(jnp.where(at_ref, s_i, 0.0))
+    diag = column_sum(jnp.where(eye, xh_r, 0.0))
+    first = group_totals(
         jnp.concatenate(
             [
                 jnp.broadcast_to(diag, (8, 128)),
@@ -115,21 +133,18 @@
                 m_i * sref_r - m_r * sref_i,
             ],
             axis=0,
-        ),
-        ones,
+        )
     )
     inv_tau = 1.0 / first[0:1]
     c_r, c_i = first[8:40], first[40:72]
     w_r = conj_c_r * inv_tau
     w_i = -conj_c_i * inv_tau
-    right_c = complex_right(cb_r, -cb_i)
-    row8 = jnp.broadcast_to(jnp.concatenate([w_r, w_i], axis=1), (8, 256))
-    cw = dot_f32(row8, right_c)
-    g_r = GRAD_SCALE * (cw[0:1, :128] - d_r)
-    g_i = GRAD_SCALE * (cw[0:1, 128:] - d_i)
+    h_r, h_i = c_r * inv_tau, c_i * inv_tau
+    g_r = GRAD_SCALE * (column_sum(h_r * k_r - h_i * k_neg) - d_r)
+    g_i = GRAD_SCALE * (column_sum(h_i * k_r + h_r * k_neg) - d_i)
     gc_r, gc_i = g_r * inv_tau, g_i * inv_tau
     gw = (g_r * w_r + g_i * w_i) * inv_tau
-    second = dot_f32(
+    second = group_totals(
         jnp.concatenate(
             [
                 jnp.broadcast_to(gw, (8, 128)),
@@ -137,21 +152,17 @@
                 m_r * gc_i + m_i * gc_r,
             ],
             axis=0,
-        ),
-        ones,
+        )
     )
     gt2 = -2.0 * second[0:1]
     u_r, u_i = second[8:40], second[40:72]
-    right_xh = complex_right(diagonal_blocks(xh_r), diagonal_blocks(xh_i))
-    q = dot_f32(jnp.concatenate([m_r, m_i], axis=1), right_xh)
-    uh8 = jnp.broadcast_to(jnp.concatenate([gc_r, -gc_i], axis=1), (8, 256))
-    uh = dot_f32(uh8, right_m)
-    uh_r, uh_i = uh[0:1, :128], uh[0:1, 128:]
+    uh_r = column_sum(jnp.where(eye, u_r, 0.0))
+    uh_i = -column_sum(jnp.where(eye, u_i, 0.0))
     col_ref = (lane % 32) == pick
     p_r = jnp.where(col_ref, u_r, 0.0) + jnp.where(at_ref, uh_r, 0.0) + gt2 * m_r
     p_i = jnp.where(col_ref, u_i, 0.0) + jnp.where(at_ref, uh_i, 0.0) + gt2 * m_i
-    n_r = (u_r * conj_c_r - u_i * conj_c_i) + (c_r * uh_r - c_i * uh_i) + gt2 * q[:, :128]
-    n_i = (u_r * conj_c_i + u_i * conj_c_r) + (c_r * uh_i + c_i * uh_r) + gt2 * q[:, 128:]
+    n_r = (u_r * conj_c_r - u_i * conj_c_i) + (c_r * uh_r - c_i * uh_i) + gt2 * q_r
+    n_i = (u_r * conj_c_i + u_i * conj_c_r) + (c_r * uh_i + c_i * uh_r) + gt2 * q_i
     upper = row <= lane % 32
     speech = jnp.where(upper, p_r, p_i) * inv_t
     noise = jnp.where(upper, n_r, n_i) * (-inv_t)
@@ -182,8 +193,9 @@
 
 
 def body(
-    wave_ref, filt_ref, smask_ref, nmask_ref, target_ref, pick_ref,
-    enh_ref, grad_ref,
+    wave_in, filt_in, smask_in, nmask_in, target_in, pick_ref,
+    enh_out, grad_ref,
+    wave_ref, filt_ref, smask_ref, nmask_ref, target_ref, enh_ref, in_sem,
     wblk, head, gath, heads, frames, zz, yy, lhs, sb, rb, pay, sgq, fg, tt, ms, mn, fb,
     g_send, g_recv, h_send, h_recv, s_send, s_recv, p_send, p_recv, f_send, f_recv,
 ):
@@ -218,6 +230,18 @@
             device_id={"dp": dev_d, "mic": dev_m}, device_id_type=pl.DeviceIdType.MESH,
         )
 
+    loads = [
+        pltpu.make_async_copy(src, dst, in_sem.at[k])
+        for k, (src, dst) in enumerate(
+            [
+                (wave_in, wave_ref), (filt_in, filt_ref), (smask_in, smask_ref),
+                (nmask_in, nmask_ref), (target_in, target_ref),
+            ]
+        )
+    ]
+    for load in loads:
+        load.start()
+
     barrier = pltpu.get_barrier_semaphore()
 
     def greet(dev_d, dev_m):
@@ -230,6 +254,9 @@
         greet(d, other_m(j))
     for peer in others + [core, prev, nxt]:
         greet(peer, mu)
+
+    for load in loads:
+        load.wait()
 
     turn = iota((128, 1024), 0)
     lane = iota((128, 1024), 1)
@@ -405,7 +432,7 @@
     def pay_copy(o, sem, dev):
         return remote(pay.at[o], pay.at[o], p_send.at[sem], p_recv.at[o], dev, mu)
 
-    for k, dev in enumerate([core] + others):
+    for k, dev in enumerate([core, others[0]] + others[:0:-1]):
         pay_copy(d, k, dev).start()
 
     def group_grads(o):
@@ -453,8 +480,8 @@
                 ).astype(BF16)
 
     spread = [
-        [(0, 0, 0), (0, 1, 0), (3, 0, 0), (1, 1, 0), (1, 0, 1), (2, 0, 0), (1, 1, 1), (2, 0, 1)],
-        [(0, 0, 1), (1, 0, 0), (0, 1, 1), (3, 1, 0), (3, 0, 1), (2, 1, 0), (3, 1, 1), (2, 1, 1)],
+        [(0, 0, 0), (0, 1, 0), (2, 0, 0), (1, 1, 0), (2, 0, 1), (1, 0, 0), (1, 1, 1), (1, 0, 1)],
+        [(0, 0, 1), (0, 1, 1), (2, 1, 0), (3, 1, 0), (2, 1, 1), (3, 0, 0), (3, 1, 1), (3, 0, 1)],
     ]
 
     @pl.loop(0, DP // 2)
@@ -478,6 +505,8 @@
         for o, dc in pair:
             group_grads(o)
 
+    enh_copy = pltpu.make_async_copy(enh_ref, enh_out, in_sem.at[5])
+    enh_copy.start()
     acc = nt_dot(sgq[...], frames[...])
     keep = iota((512, 256), 0) % 8 == (iota((512, 256), 1) % 128) // 16
     rows = jnp.sum(jnp.where(keep, acc, 0.0).reshape(64, 8, 256), axis=1)
@@ -507,6 +536,7 @@
     turned = result.T
     grad_ref[...] = jnp.concatenate([turned[32 * p : 32 * p + 32] for p in range(4)], axis=1)
 
+    enh_copy.wait()
     head_first().wait_send()
     for j in range(1, MIC):
         wave_copy(0, j, mu, mu).wait_send()
@@ -524,6 +554,7 @@
 
 def local(waveform, filters, speech_mask, noise_mask, target, ref_mic):
     vmem = pl.BlockSpec(memory_space=pltpu.VMEM)
+    anywhere = pl.BlockSpec(memory_space=pl.ANY)
     dma = pltpu.SemaphoreType.DMA
     enhanced, grad = pl.pallas_call(
         body,
@@ -531,9 +562,16 @@
             jax.ShapeDtypeStruct((2, 2, 32, TD), F32),
             jax.ShapeDtypeStruct((32, 64), F32),
         ),
-        in_specs=[vmem] * 5 + [pl.BlockSpec(memory_space=pltpu.SMEM)],
-        out_specs=(vmem, vmem),
+        in_specs=[anywhere] * 5 + [pl.BlockSpec(memory_space=pltpu.SMEM)],
+        out_specs=(anywhere, vmem),
         scratch_shapes=[
+            pltpu.VMEM((2, 4, 16 * TD), BF16),
+            pltpu.VMEM((32, 64), BF16),
+            pltpu.VMEM((2, 32, TD), BF16),
+            pltpu.VMEM((2, 32, TD), BF16),
+            pltpu.VMEM((2, 2, 32, TD), F32),
+            pltpu.VMEM((2, 2, 32, TD), F32),
+            dma((6,)),
             pltpu.VMEM((2, 64, TD), BF16),
             pltpu.VMEM((8, 128), F32),
             pltpu.VMEM((MIC, 2, 64, TD), BF16),

time: 52.5 us -> 51.8 us (0.987)
  Pallas kernels: 49.6 us -> 48.8 us
    pallas_call x1, Pallas kernels: 49.6 us -> 48.8 us  [local(): pl.pallas_call(body, out_shape=(jax.ShapeDtypeStruct((2, 2, 32, TD), F32)...]
where the time goes in v5:
time: 51.8 us; the launch traced here: 51.6 us
  Pallas kernels  48.8 us (94%)
  local copies, waits for them, and re-layouts  2.18 us (4%)
  between operations  0.65 us (1%)
    pallas_call x1, Pallas kernels, local(): pl.pallas_call(body, out_shape=(jax.ShapeDtypeStruct((2, 2, 32, TD), F32)...  48.8 us
    unnamed x4, local copies, waits for them, and re-layouts  2.18 us

profile of v5, /device:TPU:1, one launch (start us, length us, event | category | flops | bytes accessed | tf_op | source)
XLA Modules:
  0.0 51.6 jit_solution(6584137369099584254)
XLA Ops:
  0.6 48.8 %shard_map.77 = (f32[2,2,32,256]{3,2,1,0:T(8,128)}, f32[32,64]{1,0:T(8,128)}) custom-call(bf16[2,4,4096]{2,1,0:T(4,128)(2,1)} %wave_in.1, bf16[32,64]{1,0:T(8,128)(2,1)} %bitcast.3, bf16[2,32,256]{2,1,0:T(8,128)(2,1)} %smask_in.1, bf16[2,32,256]{2,1,0:T(8,128)(2,1)} %nmask_in.1, f32[2,2,32,256]{3,2,1,0:T(8,128)} %target_in.1, s32[2]{0:T(128)} %pick_ref.1), custom_call_target="tpu_custom_call" | custom-call | tf_op jit(solution)/shard_map/pallas_call | solution.py:559
  49.4 0.0 copy-start
  49.4 1.6 %copy.10 = f32[2,2,32,256]{3,2,1,0:T(8,128)} copy(f32[2,2,32,256]{3,2,1,0:T(8,128)} %get-tuple-element.8) | data formatting | bytes 262144
  51.0 0.0 copy-done
  51.0 0.6 %copy.11 = f32[64,32]{0,1:T(8,128)} copy(f32[64,32]{0,1:T(8,128)S(1)} %bitcast.2) | data formatting | bytes 16384
Async XLA Ops:
  49.4 1.6 %copy-start = (f32[32,64]{1,0:T(8,128)S(1)}, f32[32,64]{1,0:T(8,128)}, u32[]{:S(2)}) copy-start(f32[32,64]{1,0:T(8,128)} %get-tuple-element.5) | copy-start | bytes 24580

commit v6 on v5

--- a/solution.py
+++ b/solution.py
@@ -193,9 +193,9 @@
 
 
 def body(
-    wave_in, filt_in, smask_in, nmask_in, target_in, pick_ref,
+    wave_in, filt_in, smask_in, nmask_in, target_in, pick_in,
     enh_out, grad_ref,
-    wave_ref, filt_ref, smask_ref, nmask_ref, target_ref, enh_ref, in_sem,
+    wave_ref, filt_ref, smask_ref, nmask_ref, target_ref, pick_ref, enh_ref, in_sem,
     wblk, head, gath, heads, frames, zz, yy, lhs, sb, rb, pay, sgq, fg, tt, ms, mn, fb,
     g_send, g_recv, h_send, h_recv, s_send, s_recv, p_send, p_recv, f_send, f_recv,
 ):
@@ -203,12 +203,12 @@
     mu = lax.axis_index("mic")
     prev = lax.rem(d + DP - 1, DP)
     nxt = lax.rem(d + 1, DP)
-    at_z, at_x, at_c = d // 4, (d // 2) % 2, d % 2
-    chip = d // 2
-    core = 2 * chip + 1 - at_c
+    at_z, at_x, at_c = d >> 2, (d >> 1) & 1, d & 1
+    chip = d >> 1
+    core = d ^ 1
 
     def rel(dz, dx, dc):
-        return ((at_z + dz) % 4) * 4 + ((at_x + dx) % 2) * 2 + (at_c + dc) % 2
+        return ((d + 4 * dz) & 12) | ((d ^ (2 * dx + dc)) & 3)
 
     others = [rel(0, 1, 0), rel(1, 0, 0), rel(3, 0, 0), rel(1, 1, 0), rel(3, 1, 0), rel(2, 0, 0), rel(2, 1, 0)]
 
@@ -235,7 +235,7 @@
         for k, (src, dst) in enumerate(
             [
                 (wave_in, wave_ref), (filt_in, filt_ref), (smask_in, smask_ref),
-                (nmask_in, nmask_ref), (target_in, target_ref),
+                (nmask_in, nmask_ref), (target_in, target_ref), (pick_in, pick_ref),
             ]
         )
     ]
@@ -381,11 +381,11 @@
             for j in range(1, MIC):
                 head_copy(j, other_m(j), mu).wait_recv()
         encode(b)
-        here = jnp.where(at_z // 2 == b, 1, 0)
+        here = jnp.where((at_z >> 1) == b, 1, 0)
 
         def target(k, mine):
-            to = 2 * (2 * b + (at_z + k // 2 + here) % 2) + (at_x + 1 + k) % 2
-            return to, 2 * to + (at_c + 1 + mine) % 2
+            to = 4 * b + 2 * ((at_z + (k >> 1) + here) & 1) + ((at_x + 1 + k) & 1)
+            return to, 2 * to + ((at_c + 1 + mine) & 1)
 
         def give(to, o):
             sum_copy(o, to, to, core).start()
@@ -421,7 +421,7 @@
                 keep(to_b, o_b)
 
     for k in range(7):
-        add_slot(d, 8 + others[k] // 2)
+        add_slot(d, 8 + (others[k] >> 1))
     pick = jnp.where(d < DP // 2, pick_ref[0], pick_ref[1])
     speech, noise, w_r, w_i = solve(sb[d], pick)
     left_half = lane32 < 64
@@ -436,8 +436,8 @@
         pay_copy(d, k, dev).start()
 
     def group_grads(o):
-        b = o // 8
-        f0 = (o % 8) * 4
+        b = o >> 3
+        f0 = (o & 7) << 2
         w_r = jnp.where(own8, pay[o, 64:65, :], 0.0)
         w_i = jnp.where(own8, pay[o, 65:66, :], 0.0)
         wr_hi, wr_lo = split(w_r)
@@ -488,10 +488,8 @@
     def _(i):
         pair = []
         for column in spread:
-            dz = table(i, [k[0] for k in column])
-            dx = table(i, [k[1] for k in column])
-            dc = table(i, [k[2] for k in column])
-            pair.append((rel(dz, dx, dc), dc))
+            code = table(i, [4 * k[0] + 2 * k[1] + k[2] for k in column])
+            pair.append((((d + (code & 12)) & 12) | ((d ^ code) & 3), code & 1))
         for o, dc in pair:
 
             @pl.when(o != d)
@@ -500,12 +498,12 @@
 
             @pl.when((o != d) & (dc == 0))
             def _():
-                pay_copy(o, 8 + o // 2, core).start()
+                pay_copy(o, 8 + (o >> 1), core).start()
 
         for o, dc in pair:
             group_grads(o)
 
-    enh_copy = pltpu.make_async_copy(enh_ref, enh_out, in_sem.at[5])
+    enh_copy = pltpu.make_async_copy(enh_ref, enh_out, in_sem.at[6])
     enh_copy.start()
     acc = nt_dot(sgq[...], frames[...])
     keep = iota((512, 256), 0) % 8 == (iota((512, 256), 1) % 128) // 16
@@ -546,13 +544,17 @@
         sum_copy(d, 0, k, core).wait_send()
         pay_copy(d, k, core).wait_send()
     for k in range(7):
-        sum_copy(d, 0, 8 + others[k] // 2, core).wait_send()
-        pay_copy(d, 8 + others[k] // 2, core).wait_send()
+        sum_copy(d, 0, 8 + (others[k] >> 1), core).wait_send()
+        pay_copy(d, 8 + (others[k] >> 1), core).wait_send()
     for j in range(1, DP):
         grad_copy(j, d, d).wait_send()
 
 
 def local(waveform, filters, speech_mask, noise_mask, target, ref_mic):
+    held = [
+        pltpu.with_memory_space_constraint(v, pltpu.HBM)
+        for v in (waveform, filters.T, speech_mask, noise_mask, target, ref_mic)
+    ]
     vmem = pl.BlockSpec(memory_space=pltpu.VMEM)
     anywhere = pl.BlockSpec(memory_space=pl.ANY)
     dma = pltpu.SemaphoreType.DMA
@@ -562,7 +564,7 @@
             jax.ShapeDtypeStruct((2, 2, 32, TD), F32),
             jax.ShapeDtypeStruct((32, 64), F32),
         ),
-        in_specs=[anywhere] * 5 + [pl.BlockSpec(memory_space=pltpu.SMEM)],
+        in_specs=[pl.BlockSpec(memory_space=pltpu.HBM)] * 6,
         out_specs=(anywhere, vmem),
         scratch_shapes=[
             pltpu.VMEM((2, 4, 16 * TD), BF16),
@@ -570,8 +572,9 @@
             pltpu.VMEM((2, 32, TD), BF16),
             pltpu.VMEM((2, 32, TD), BF16),
             pltpu.VMEM((2, 2, 32, TD), F32),
+            pltpu.SMEM((2,), jnp.int32),
             pltpu.VMEM((2, 2, 32, TD), F32),
-            dma((6,)),
+            dma((7,)),
             pltpu.VMEM((2, 64, TD), BF16),
             pltpu.VMEM((8, 128), F32),
             pltpu.VMEM((MIC, 2, 64, TD), BF16),
@@ -593,9 +596,9 @@
             dma((DP,)), dma((DP,)), dma((DP,)), dma((DP,)), dma((DP,)), dma((DP,)),
         ],
         compiler_params=pltpu.CompilerParams(
-            collective_id=0, has_side_effects=True, vmem_limit_bytes=60 * 1024 * 1024
+            collective_id=0, has_side_effects=True, vmem_limit_bytes=28 * 1024 * 1024
         ),
-    )(waveform, filters.T, speech_mask, noise_mask, target, ref_mic)
+    )(*held)
     return (enhanced, grad.T)
 
 

time: 51.8 us -> 49.6 us (0.958)
  Pallas kernels: 48.8 us -> 47.6 us
  local copies, waits for them, and re-layouts: 2.18 us -> 1.26 us
    pallas_call x1, Pallas kernels: 48.8 us -> 47.6 us  [local(): pl.pallas_call(body, out_shape=(jax.ShapeDtypeStruct((2, 2, 32, TD), F32)...]
    unnamed x4 -> x2, local copies, waits for them, and re-layouts: 2.18 us -> 1.26 us
where the time goes in v6:
time: 49.6 us; the launch traced here: 49.5 us
  Pallas kernels  47.6 us (96%)
  local copies, waits for them, and re-layouts  1.26 us (3%)
  between operations  0.64 us (1%)
    pallas_call x1, Pallas kernels, local(): pl.pallas_call(body, out_shape=(jax.ShapeDtypeStruct((2, 2, 32, TD), F32)...  47.6 us
    unnamed x2, local copies, waits for them, and re-layouts  1.26 us

profile of v6, /device:TPU:1, one launch (start us, length us, event | category | flops | bytes accessed | tf_op | source)
XLA Modules:
  0.0 49.5 jit_solution(15901511004377913681)
XLA Ops:
  0.6 47.6 %shard_map.77 = (f32[2,2,32,256]{3,2,1,0:T(8,128)S(1)}, f32[32,64]{1,0:T(8,128)S(1)}) custom-call(bf16[2,4,4096]{2,1,0:T(4,128)(2,1)} %wave_in.1, bf16[32,64]{1,0:T(8,128)(2,1)} %bitcast.3, bf16[2,32,256]{2,1,0:T(8,128)(2,1)} %smask_in.1, bf16[2,32,256]{2,1,0:T(8,128)(2,1)} %nmask_in.1, f32[2,2,32,256]{3,2,1,0:T(8,128)} %target_in.1, s32[2]{0:T(128)} %pick_in.1), custom_call_target="tpu_custom_call" | custom-call | tf_op jit(solution)/shard_map/pallas_call | solution.py:561
  48.2 0.7 %copy.10 = f32[2,2,32,256]{3,2,1,0:T(8,128)} copy(f32[2,2,32,256]{3,2,1,0:T(8,128)S(1)} %get-tuple-element.8) | data formatting | bytes 262144
  48.9 0.6 %copy.11 = f32[64,32]{0,1:T(8,128)} copy(f32[64,32]{0,1:T(8,128)S(1)} %bitcast.2) | data formatting | bytes 16384

commit v7 on v6

--- a/solution.py
+++ b/solution.py
@@ -101,7 +101,7 @@
     return out[0:n] + (out[n : 2 * n] + out[2 * n :])
 
 
-def solve(total, pick):
+def solve(total, late, pick):
     lane = iota((32, 128), 1)
     row = iota((32, 128), 0)
     eye = row == lane % 32
@@ -112,8 +112,6 @@
 
     s_r, s_neg = unpack_four(total[0:32])
     n_r, n_neg = unpack_four(total[32:64])
-    k_r, k_neg = unpack_four(total[64:96])
-    d_r, d_i = total[96:97], total[97:98]
     s_r = s_r * inv_t + jnp.where(eye, LOAD, 0.0)
     s_i = s_neg * -inv_t
     m_r, m_i = inverse(n_r * inv_t + jnp.where(eye, LOAD, 0.0), n_neg * -inv_t)
@@ -140,6 +138,9 @@
     w_r = conj_c_r * inv_tau
     w_i = -conj_c_i * inv_tau
     h_r, h_i = c_r * inv_tau, c_i * inv_tau
+    rest = late()
+    k_r, k_neg = unpack_four(rest[0:32])
+    d_r, d_i = rest[32:33], rest[33:34]
     g_r = GRAD_SCALE * (column_sum(h_r * k_r - h_i * k_neg) - d_r)
     g_i = GRAD_SCALE * (column_sum(h_i * k_r + h_r * k_neg) - d_i)
     gc_r, gc_i = g_r * inv_tau, g_i * inv_tau
@@ -339,10 +340,16 @@
     row8 = iota((8, 128), 0)
     own8 = row8 == iota((8, 128), 1) // 32
 
-    def group_sums(o, w):
-        t_hi, t_lo = split(tt[o])
-        lhs[w, 512:768, :] = zz[o].reshape(256, TD)
-        lhs[w, 768:800, :] = jnp.concatenate([t_hi, t_lo], axis=0).astype(BF16)
+    def packed(out, first):
+        value = jnp.zeros((32, 128), F32)
+        for g in range(4):
+            re = out[first + 32 * g : first + 32 * g + 32]
+            im = out[first + 128 + 32 * g : first + 160 + 32 * g]
+            one = jnp.where(upper, re[:, :128] + im[:, 128:], im[:, :128] - re[:, 128:])
+            value = jnp.where(lane32 // 32 == g, one, value)
+        return value
+
+    def masked_sums(o, w):
         for g in range(4):
             for k, ref in enumerate((ms, mn)):
                 mask = jnp.broadcast_to(ref[pl.ds(4 * o + g, 1), :], (32, TD)).astype(BF16)
@@ -353,26 +360,72 @@
                     row = 64 * k + 32 * ((v + g) % 2)
                     yy[o, g, row : row + 32, :] = part
         out = nt_dot(lhs[w], zz[o].reshape(256, TD))
-        for kind in range(3):
-            value = jnp.zeros((32, 128), F32)
-            for g in range(4):
-                re = out[256 * kind + 32 * g : 256 * kind + 32 * g + 32]
-                im = out[256 * kind + 128 + 32 * g : 256 * kind + 160 + 32 * g]
-                one = jnp.where(upper, re[:, :128] + im[:, 128:], im[:, :128] - re[:, 128:])
-                value = jnp.where(lane32 // 32 == g, one, value)
-            sb[o, 32 * kind : 32 * kind + 32, :] = value
-        t0 = out[768:776] + out[784:792]
-        t1 = out[776:784] + out[792:800]
+        sb[o, 0:32, :] = packed(out, 0)
+        sb[o, 32:64, :] = packed(out, 256)
+
+    def other_sums(o, w):
+        t_hi, t_lo = split(tt[o])
+        own = zz[o].reshape(256, TD)
+        t_rows = jnp.concatenate([t_hi, t_lo], axis=0).astype(BF16)
+        out = nt_dot(jnp.concatenate([own, t_rows], axis=0), own)
+        sb[o, 64:96, :] = packed(out, 0)
+        t0 = out[256:264] + out[272:280]
+        t1 = out[264:272] + out[280:288]
         d_r = jnp.sum(jnp.where(own8, t0[:, :128] + t1[:, 128:], 0.0), axis=0, keepdims=True)
         d_i = jnp.sum(jnp.where(own8, t0[:, 128:] - t1[:, :128], 0.0), axis=0, keepdims=True)
         sb[o, 96:104, :] = jnp.where(row8 == 0, d_r, jnp.where(row8 == 1, d_i, 0.0))
 
-    def sum_copy(o, slot, sem, dev):
-        return remote(sb.at[o], rb.at[slot], s_send.at[sem], s_recv.at[slot], dev, mu)
-
-    def add_slot(o, slot):
-        sum_copy(o, slot, slot, core).wait_recv()
-        sb[o] = sb[o] + rb[slot]
+    def sum_copy(n, o, slot, sem, dev):
+        rows = slice(0, 64) if n == 0 else slice(64, ROWS)
+        return remote(
+            sb.at[o, rows], rb.at[slot, rows], s_send.at[DP * n + sem], s_recv.at[DP * n + slot],
+            dev, mu,
+        )
+
+    def add_slot(n, o, slot):
+        rows = slice(0, 64) if n == 0 else slice(64, ROWS)
+        sum_copy(n, o, slot, slot, core).wait_recv()
+        sb[o, rows, :] = sb[o, rows, :] + rb[slot, rows, :]
+
+    def pass_over(n, b, sums):
+        here = jnp.where((at_z >> 1) == b, 1, 0)
+
+        def target(k, mine):
+            to = 4 * b + 2 * ((at_z + (k >> 1) + here) & 1) + ((at_x + 1 + k) & 1)
+            return to, 2 * to + ((at_c + 1 + mine) & 1)
+
+        def give(to, o):
+            sum_copy(n, o, to, to, core).start()
+
+        def keep(to, o):
+            add_slot(n, o, to)
+
+            @pl.when(to != chip)
+            def _():
+                sum_copy(n, o, 8 + chip, 8 + to, o).start()
+
+        @pl.loop(0, 4)
+        def _(i):
+            to_a, o_a = target(table(i, [0, 2, 3, 2]), table(i, [0, 0, 0, 1]))
+            to_b, o_b = target(table(i, [1, 0, 1, 3]), table(i, [0, 1, 1, 1]))
+            sums(o_a, 0)
+            sums(o_b, 1)
+
+            @pl.when(i < 3)
+            def _():
+                give(to_a, o_a)
+
+            @pl.when(i == 3)
+            def _():
+                keep(to_a, o_a)
+
+            @pl.when(i == 0)
+            def _():
+                give(to_b, o_b)
+
+            @pl.when(i > 0)
+            def _():
+                keep(to_b, o_b)
 
     for b in range(2):
         for j in range(1, MIC):
@@ -381,49 +434,17 @@
             for j in range(1, MIC):
                 head_copy(j, other_m(j), mu).wait_recv()
         encode(b)
-        here = jnp.where((at_z >> 1) == b, 1, 0)
-
-        def target(k, mine):
-            to = 4 * b + 2 * ((at_z + (k >> 1) + here) & 1) + ((at_x + 1 + k) & 1)
-            return to, 2 * to + ((at_c + 1 + mine) & 1)
-
-        def give(to, o):
-            sum_copy(o, to, to, core).start()
-
-        def keep(to, o):
-            add_slot(o, to)
-
-            @pl.when(to != chip)
-            def _():
-                sum_copy(o, 8 + chip, 8 + to, o).start()
-
-        @pl.loop(0, 4)
-        def _(i):
-            to_a, o_a = target(table(i, [0, 2, 3, 2]), table(i, [0, 0, 0, 1]))
-            to_b, o_b = target(table(i, [1, 0, 1, 3]), table(i, [0, 1, 1, 1]))
-            group_sums(o_a, 0)
-            group_sums(o_b, 1)
-
-            @pl.when(i < 3)
-            def _():
-                give(to_a, o_a)
-
-            @pl.when(i == 3)
-            def _():
-                keep(to_a, o_a)
-
-            @pl.when(i == 0)
-            def _():
-                give(to_b, o_b)
-
-            @pl.when(i > 0)
-            def _():
-                keep(to_b, o_b)
-
-    for k in range(7):
-        add_slot(d, 8 + (others[k] >> 1))
+        pass_over(0, b, masked_sums)
+    for b in range(2):
+        pass_over(1, b, other_sums)
+
+    def collect(n):
+        for k in range(7):
+            add_slot(n, d, 8 + (others[k] >> 1))
+        return sb[d, 0:64, :] if n == 0 else sb[d, 64:ROWS, :]
+
     pick = jnp.where(d < DP // 2, pick_ref[0], pick_ref[1])
-    speech, noise, w_r, w_i = solve(sb[d], pick)
+    speech, noise, w_r, w_i = solve(collect(0), lambda: collect(1), pick)
     left_half = lane32 < 64
     pay[d, 0:32, :] = jnp.where(left_half, speech, pltpu.roll(noise, 64, axis=1))
     pay[d, 32:64, :] = jnp.where(left_half, pltpu.roll(speech, 64, axis=1), noise)
@@ -541,10 +562,12 @@
         wave_copy(1, j, mu, mu).wait_send()
         head_copy(j, mu, mu).wait_send()
     for k in range(8):
-        sum_copy(d, 0, k, core).wait_send()
+        sum_copy(0, d, 0, k, core).wait_send()
+        sum_copy(1, d, 0, k, core).wait_send()
         pay_copy(d, k, core).wait_send()
     for k in range(7):
-        sum_copy(d, 0, 8 + (others[k] >> 1), core).wait_send()
+        sum_copy(0, d, 0, 8 + (others[k] >> 1), core).wait_send()
+        sum_copy(1, d, 0, 8 + (others[k] >> 1), core).wait_send()
         pay_copy(d, 8 + (others[k] >> 1), core).wait_send()
     for j in range(1, DP):
         grad_copy(j, d, d).wait_send()
@@ -582,7 +605,7 @@
             pltpu.VMEM((256, 8 * TD), BF16),
             pltpu.VMEM((DP, 2, 4, 32, TD), BF16),
             pltpu.VMEM((DP, 4, 128, TD), BF16),
-            pltpu.VMEM((2, 800, TD), BF16),
+            pltpu.VMEM((2, 512, TD), BF16),
             pltpu.VMEM((DP, ROWS, 128), F32),
             pltpu.VMEM((DP, ROWS, 128), F32),
             pltpu.VMEM((DP, PAY, 128), F32),
@@ -593,7 +616,7 @@
             pltpu.VMEM((64, TD), F32),
             pltpu.VMEM((512, 256), BF16),
             dma((2 * MIC,)), dma((2 * MIC,)), dma((MIC,)), dma((MIC,)),
-            dma((DP,)), dma((DP,)), dma((DP,)), dma((DP,)), dma((DP,)), dma((DP,)),
+            dma((2 * DP,)), dma((2 * DP,)), dma((DP,)), dma((DP,)), dma((DP,)), dma((DP,)),
         ],
         compiler_params=pltpu.CompilerParams(
             collective_id=0, has_side_effects=True, vmem_limit_bytes=28 * 1024 * 1024

time: 49.6 us -> 49.3 us (level)
  no operation moved by 1% of the time
where the time goes in v7:
time: 49.3 us; the launch traced here: 49.1 us
  Pallas kernels  47.2 us (96%)
  local copies, waits for them, and re-layouts  1.26 us (3%)
  between operations  0.64 us (1%)
    pallas_call x1, Pallas kernels, local(): pl.pallas_call(body, out_shape=(jax.ShapeDtypeStruct((2, 2, 32, TD), F32)...  47.2 us
    unnamed x2, local copies, waits for them, and re-layouts  1.26 us

profile of v7, /device:TPU:1, one launch (start us, length us, event | category | flops | bytes accessed | tf_op | source)
XLA Modules:
  0.0 49.1 jit_solution(13143265296840442516)
XLA Ops:
  0.6 47.2 %shard_map.77 = (f32[2,2,32,256]{3,2,1,0:T(8,128)S(1)}, f32[32,64]{1,0:T(8,128)S(1)}) custom-call(bf16[2,4,4096]{2,1,0:T(4,128)(2,1)} %wave_in.1, bf16[32,64]{1,0:T(8,128)(2,1)} %bitcast.3, bf16[2,32,256]{2,1,0:T(8,128)(2,1)} %smask_in.1, bf16[2,32,256]{2,1,0:T(8,128)(2,1)} %nmask_in.1, f32[2,2,32,256]{3,2,1,0:T(8,128)} %target_in.1, s32[2]{0:T(128)} %pick_in.1), custom_call_target="tpu_custom_call" | custom-call | tf_op jit(solution)/shard_map/pallas_call | solution.py:584
  47.9 0.7 %copy.10 = f32[2,2,32,256]{3,2,1,0:T(8,128)} copy(f32[2,2,32,256]{3,2,1,0:T(8,128)S(1)} %get-tuple-element.8) | data formatting | bytes 262144
  48.5 0.6 %copy.11 = f32[64,32]{0,1:T(8,128)} copy(f32[64,32]{0,1:T(8,128)S(1)} %bitcast.2) | data formatting | bytes 16384

commit v8 on v7

--- a/solution.py
+++ b/solution.py
@@ -306,11 +306,17 @@
 
     last = d == DP - 1
     tap128 = iota((128, 128), 1) == iota((128, 128), 0) % 16
-    end = iota((128, TD), 1) == TD - 1
+    end = iota((128, 128), 1) == 127
+
+    def prepare(b):
+        for q in range(4):
+            x = jnp.concatenate([gath[2 * q, b], gath[2 * q + 1, b]], axis=0).astype(F32)
+            piece = slice(TD * (4 * b + q), TD * (4 * b + q) + TD)
+            frames[0:128, piece] = x.astype(BF16)
+            frames[128:256, piece] = pltpu.roll(x, TD - 1, axis=1).astype(BF16)
 
     def encode(b):
         for q in range(4):
-            x = jnp.concatenate([gath[2 * q, b], gath[2 * q + 1, b]], axis=0).astype(F32)
             near = jnp.concatenate(
                 [
                     jnp.broadcast_to(heads[2 * q + p, 4 * b + m : 4 * b + m + 1, :], (16, 128))
@@ -321,10 +327,9 @@
             )
             near = jnp.where(last, 0.0, near)
             column = jnp.sum(jnp.where(tap128, near, 0.0), axis=1, keepdims=True)
-            moved = jnp.where(end, column, pltpu.roll(x, TD - 1, axis=1))
-            piece = slice(TD * (4 * b + q), TD * (4 * b + q) + TD)
-            frames[0:128, piece] = x.astype(BF16)
-            frames[128:256, piece] = moved.astype(BF16)
+            piece = slice(TD * (4 * b + q) + 128, TD * (4 * b + q) + TD)
+            tail = frames[128:256, piece].astype(F32)
+            frames[128:256, piece] = jnp.where(end, column, tail).astype(BF16)
         for half in range(2):
             at = TD * (4 * b + 2 * half)
             a0 = jnp.dot(fb[...], frames[:, at : at + TD], preferred_element_type=F32)
@@ -430,6 +435,7 @@
     for b in range(2):
         for j in range(1, MIC):
             wave_copy(b, j, other_m(j), mu).wait_recv()
+        prepare(b)
         if b == 0:
             for j in range(1, MIC):
                 head_copy(j, other_m(j), mu).wait_recv()

time: 49.3 us -> 49 us (level)
  no operation moved by 1% of the time
where the time goes in v8:
time: 49 us; the launch traced here: 48.8 us
  Pallas kernels  46.9 us (96%)
  local copies, waits for them, and re-layouts  1.26 us (3%)
  between operations  0.64 us (1%)
    pallas_call x1, Pallas kernels, local(): pl.pallas_call(body, out_shape=(jax.ShapeDtypeStruct((2, 2, 32, TD), F32)...  46.9 us
    unnamed x2, local copies, waits for them, and re-layouts  1.26 us

profile of v8, /device:TPU:1, one launch (start us, length us, event | category | flops | bytes accessed | tf_op | source)
XLA Modules:
  0.0 48.8 jit_solution(2555573516445350359)
XLA Ops:
  0.6 46.9 %shard_map.77 = (f32[2,2,32,256]{3,2,1,0:T(8,128)S(1)}, f32[32,64]{1,0:T(8,128)S(1)}) custom-call(bf16[2,4,4096]{2,1,0:T(4,128)(2,1)} %wave_in.1, bf16[32,64]{1,0:T(8,128)(2,1)} %bitcast.3, bf16[2,32,256]{2,1,0:T(8,128)(2,1)} %smask_in.1, bf16[2,32,256]{2,1,0:T(8,128)(2,1)} %nmask_in.1, f32[2,2,32,256]{3,2,1,0:T(8,128)} %target_in.1, s32[2]{0:T(128)} %pick_in.1), custom_call_target="tpu_custom_call" | custom-call | tf_op jit(solution)/shard_map/pallas_call | solution.py:590
  47.6 0.7 %copy.10 = f32[2,2,32,256]{3,2,1,0:T(8,128)} copy(f32[2,2,32,256]{3,2,1,0:T(8,128)S(1)} %get-tuple-element.8) | data formatting | bytes 262144
  48.2 0.6 %copy.11 = f32[64,32]{0,1:T(8,128)} copy(f32[64,32]{0,1:T(8,128)S(1)} %bitcast.2) | data formatting | bytes 16384
